TPU v7x, 32 devices: a whole 2x2x4 slice. The times are simulated.
32 devices in a mesh: rep: 4 (over y, x), shard: 8 (over z, core).
Axes of the slice: x: 2, y: 2, z: 4, core: 2. Of those that a mesh axis runs over, the one named last changes fastest.
Arguments:
- layer_input: bfloat16 [32, 1024, 768], P(('rep', 'shard')), may hold values from -6 to 6
- segment_ids: int32 [32, 1024], P(('rep', 'shard')), may hold values from 0 to 5, never falling along the last dimension, each value on 1 to 800 neighbouring positions
- cotangent: bfloat16 [32, 1024, 768], P(('rep', 'shard')), may hold values from -6 to 6
- w_qkv: bfloat16 [768, 2304], P('shard'), may hold values from -0.21875 to 0.21875
- bias_query: bfloat16 [768], P('shard'), may hold values from -3 to 3
- bias_value: bfloat16 [768], P('shard'), may hold values from -3 to 3
- w_out: bfloat16 [768, 768], P('shard'), may hold values from -0.875 to 0.875
- bias_out: bfloat16 [768], P('shard'), may hold values from -3 to 3
- ln1_gain: bfloat16 [768], P('shard'), may hold values from 0.25 to 1.75
- ln1_bias: bfloat16 [768], P('shard'), may hold values from -3 to 3
- w_up: bfloat16 [768, 3072], P('shard'), may hold values from -0.21875 to 0.21875
- bias_up: bfloat16 [3072], P('shard'), may hold values from -3 to 3
- w_down: bfloat16 [3072, 768], P('shard'), may hold values from -0.109375 to 0.109375
- bias_down: bfloat16 [768], P('shard'), may hold values from -3 to 3
- ln2_gain: bfloat16 [768], P('shard'), may hold values from 0.25 to 1.75
- ln2_bias: bfloat16 [768], P('shard'), may hold values from -3 to 3
Outputs:
- layer_output: bfloat16 [32, 1024, 768], P(('rep', 'shard'))
- input_grad: bfloat16 [32, 1024, 768], P(('rep', 'shard'))
- grad_w_qkv: float32 [768, 2304], P('shard')
- grad_bias_query: float32 [768], P('shard')
- grad_bias_value: float32 [768], P('shard')
- grad_w_out: float32 [768, 768], P('shard')
- grad_bias_out: float32 [768], P('shard')
- grad_ln1_gain: float32 [768], P('shard')
- grad_ln1_bias: float32 [768], P('shard')
- grad_w_up: float32 [768, 3072], P('shard')
- grad_bias_up: float32 [3072], P('shard')
- grad_w_down: float32 [3072, 768], P('shard')
- grad_bias_down: float32 [768], P('shard')
- grad_ln2_gain: float32 [768], P('shard')
- grad_ln2_bias: float32 [768], P('shard')
Inputs may be any that keep to these rules, and one draw needn't show every extreme that they name: `segment_ids`: document numbers never fall along a sequence; each document holds 1 to 800 tokens of one sequence.
All inputs are finite; a program needn't handle non-finite values.
Results may differ from a plain program's by a relative error of at most 0.02.
Values may be sent and summed in bfloat16 or wider, within the bound.
No kernel may reach another device: no remote copies, remote signals or barrier semaphores. Data moves between devices by JAX's collectives and lax.ppermute only.
A program may use at most 256 MiB of HBM per device.

v0:
```python
import math

import jax
import jax.numpy as jnp
from jax import lax
from jax.sharding import PartitionSpec as P

HEADS = 12
HEAD_DIM = 64


def layer_norm(values, gain, shift):
    centred = values - jnp.mean(values, -1, keepdims=True)
    inv_std = lax.rsqrt(jnp.mean(centred * centred, -1, keepdims=True) + 1e-12)
    normed = centred * inv_std
    return (normed * gain + shift, normed, inv_std)


def norm_back(grad_out, normed, inv_std, gain):
    scaled = grad_out * gain
    grad_in = inv_std * (
        scaled
        - jnp.mean(scaled, -1, keepdims=True)
        - normed * jnp.mean(scaled * normed, -1, keepdims=True)
    )
    return (grad_in, jnp.sum(grad_out * normed, 0), jnp.sum(grad_out, 0))


def gelu_exact(values):
    return 0.5 * values * (1.0 + lax.erf(values * (1.0 / math.sqrt(2.0))))


def gelu_slope(values):
    return 0.5 * (1.0 + lax.erf(values * (1.0 / math.sqrt(2.0)))) + values * jnp.exp(
        -0.5 * values * values
    ) * (1.0 / math.sqrt(2.0 * math.pi))


def block_scores(query_rows, keys_all, segment_rows, segment_all):
    scores = (
        jnp.einsum("qhd,khd->hqk", query_rows, keys_all, preferred_element_type=jnp.float32) * 0.125
    )
    same_doc = segment_rows[:, None] == segment_all[None, :]
    return jnp.where(same_doc[None], scores, -1e30)


def attend_forward(queries, keys_all, values_all, segment_all):
    length, heads, head_size = queries.shape
    block_rows = min(512, length)
    blocks = length // block_rows

    def one_block(block_pair):
        query_rows, segment_rows = block_pair
        scores = block_scores(query_rows, keys_all, segment_rows, segment_all)
        top_score = jnp.max(scores, -1, keepdims=True)
        expo = jnp.exp(scores - top_score)
        total = jnp.sum(expo, -1, keepdims=True)
        weights = (expo / total).astype(jnp.bfloat16)
        mixed = jnp.einsum("hqk,khd->qhd", weights, values_all, preferred_element_type=jnp.float32)
        return (mixed.astype(jnp.bfloat16), (top_score + jnp.log(total))[..., 0])

    mixed, log_total = lax.map(
        one_block,
        (
            queries.reshape(blocks, block_rows, heads, head_size),
            segment_all.reshape(blocks, block_rows),
        ),
    )
    return (mixed.reshape(length, heads * head_size), log_total)


def attend_backward(queries, keys_all, values_all, grad_mixed, log_total, segment_all):
    length, heads, head_size = queries.shape
    block_rows = min(512, length)
    blocks = length // block_rows

    def one_block(carry, block_data):
        grad_keys, grad_values = carry
        query_rows, grad_rows, total_rows, segment_rows = block_data
        scores = block_scores(query_rows, keys_all, segment_rows, segment_all)
        weights = jnp.exp(scores - total_rows[..., None])
        grad_values = grad_values + jnp.einsum(
            "hqk,qhd->khd",
            weights.astype(jnp.bfloat16),
            grad_rows,
            preferred_element_type=jnp.float32,
        )
        grad_weights = jnp.einsum(
            "qhd,khd->hqk", grad_rows, values_all, preferred_element_type=jnp.float32
        )
        row_dot = jnp.sum(weights * grad_weights, -1, keepdims=True)
        grad_scores = (weights * (grad_weights - row_dot)).astype(jnp.bfloat16)
        grad_query = (
            jnp.einsum("hqk,khd->qhd", grad_scores, keys_all, preferred_element_type=jnp.float32)
            * 0.125
        )
        grad_keys = (
            grad_keys
            + jnp.einsum(
                "hqk,qhd->khd", grad_scores, query_rows, preferred_element_type=jnp.float32
            )
            * 0.125
        )
        return ((grad_keys, grad_values), grad_query)

    zero_heads = jnp.zeros((length, heads, head_size), jnp.float32)
    (grad_keys, grad_values), grad_query = lax.scan(
        one_block,
        (zero_heads, zero_heads),
        (
            queries.reshape(blocks, block_rows, heads, head_size),
            grad_mixed.reshape(blocks, block_rows, heads, head_size),
            log_total,
            segment_all.reshape(blocks, block_rows),
        ),
    )
    width = heads * head_size
    return jnp.concatenate(
        [
            grad_query.reshape(length, width),
            grad_keys.reshape(length, width),
            grad_values.reshape(length, width),
        ],
        -1,
    ).astype(jnp.bfloat16)


def body(
    layer_input,
    segment_ids,
    cotangent,
    w_qkv,
    bias_query,
    bias_value,
    w_out,
    bias_out,
    ln1_gain,
    ln1_bias,
    w_up,
    bias_up,
    w_down,
    bias_down,
    ln2_gain,
    ln2_bias,
):
    gathered = (
        lax.all_gather(w_qkv, "shard", axis=0, tiled=True),
        lax.all_gather(bias_query, "shard", axis=0, tiled=True),
        lax.all_gather(bias_value, "shard", axis=0, tiled=True),
        lax.all_gather(w_out, "shard", axis=0, tiled=True),
        lax.all_gather(bias_out, "shard", axis=0, tiled=True),
        lax.all_gather(ln1_gain, "shard", axis=0, tiled=True),
        lax.all_gather(ln1_bias, "shard", axis=0, tiled=True),
        lax.all_gather(w_up, "shard", axis=0, tiled=True),
        lax.all_gather(bias_up, "shard", axis=0, tiled=True),
        lax.all_gather(w_down, "shard", axis=0, tiled=True),
        lax.all_gather(bias_down, "shard", axis=0, tiled=True),
        lax.all_gather(ln2_gain, "shard", axis=0, tiled=True),
        lax.all_gather(ln2_bias, "shard", axis=0, tiled=True),
    )
    (
        full_qkv,
        full_query_bias,
        full_value_bias,
        full_out,
        full_out_bias,
        full_gain_one,
        full_shift_one,
        full_up,
        full_up_bias,
        full_down,
        full_down_bias,
        full_gain_two,
        full_shift_two,
    ) = gathered
    seq_count, length, width = layer_input.shape
    tokens = seq_count * length
    inputs_flat = layer_input.reshape(tokens, width)
    zeros_key = jnp.zeros((width,), jnp.float32)
    qkv_bias = jnp.concatenate(
        [full_query_bias.astype(jnp.float32), zeros_key, full_value_bias.astype(jnp.float32)]
    )
    projected = (
        jnp.dot(inputs_flat, full_qkv, preferred_element_type=jnp.float32) + qkv_bias
    ).astype(jnp.bfloat16)
    heads_all = projected.reshape(seq_count, length, 3, HEADS, HEAD_DIM)
    queries = heads_all[:, :, 0]
    keys_all = heads_all[:, :, 1]
    values_all = heads_all[:, :, 2]
    mixed, log_total = lax.map(
        lambda seq_data: attend_forward(*seq_data), (queries, keys_all, values_all, segment_ids)
    )
    mixed = mixed.reshape(tokens, width)
    hidden = (
        inputs_flat.astype(jnp.float32)
        + jnp.dot(mixed, full_out, preferred_element_type=jnp.float32)
        + full_out_bias.astype(jnp.float32)
    )
    normed_value, normed_one, inv_std_one = layer_norm(
        hidden, full_gain_one.astype(jnp.float32), full_shift_one.astype(jnp.float32)
    )
    normed_low = normed_value.astype(jnp.bfloat16)
    inner = jnp.dot(normed_low, full_up, preferred_element_type=jnp.float32) + full_up_bias.astype(
        jnp.float32
    )
    activated = gelu_exact(inner).astype(jnp.bfloat16)
    summed = (
        normed_low.astype(jnp.float32)
        + jnp.dot(activated, full_down, preferred_element_type=jnp.float32)
        + full_down_bias.astype(jnp.float32)
    )
    output_value, normed_two, inv_std_two = layer_norm(
        summed, full_gain_two.astype(jnp.float32), full_shift_two.astype(jnp.float32)
    )
    layer_output = output_value.astype(jnp.bfloat16).reshape(seq_count, length, width)
    backward_weights = (
        lax.all_gather(w_qkv, "shard", axis=0, tiled=True),
        lax.all_gather(bias_query, "shard", axis=0, tiled=True),
        lax.all_gather(bias_value, "shard", axis=0, tiled=True),
        lax.all_gather(w_out, "shard", axis=0, tiled=True),
        lax.all_gather(bias_out, "shard", axis=0, tiled=True),
        lax.all_gather(ln1_gain, "shard", axis=0, tiled=True),
        lax.all_gather(ln1_bias, "shard", axis=0, tiled=True),
        lax.all_gather(w_up, "shard", axis=0, tiled=True),
        lax.all_gather(bias_up, "shard", axis=0, tiled=True),
        lax.all_gather(w_down, "shard", axis=0, tiled=True),
        lax.all_gather(bias_down, "shard", axis=0, tiled=True),
        lax.all_gather(ln2_gain, "shard", axis=0, tiled=True),
        lax.all_gather(ln2_bias, "shard", axis=0, tiled=True),
    )
    back_qkv = backward_weights[0]
    back_out = backward_weights[3]
    back_gain_one = backward_weights[5].astype(jnp.float32)
    back_up = backward_weights[7]
    back_down = backward_weights[9]
    back_gain_two = backward_weights[11].astype(jnp.float32)
    grad_output = cotangent.reshape(tokens, width).astype(jnp.float32)
    grad_summed, grad_gain_two, grad_shift_two = norm_back(
        grad_output, normed_two, inv_std_two, back_gain_two
    )
    grad_branch_ffn = grad_summed.astype(jnp.bfloat16)
    grad_down = jnp.einsum(
        "nf,nd->fd", activated, grad_branch_ffn, preferred_element_type=jnp.float32
    )
    grad_down_bias = jnp.sum(grad_branch_ffn.astype(jnp.float32), 0)
    grad_activated = jnp.einsum(
        "nd,fd->nf", grad_branch_ffn, back_down, preferred_element_type=jnp.float32
    )
    grad_inner = (grad_activated * gelu_slope(inner)).astype(jnp.bfloat16)
    grad_up = jnp.einsum("nd,nf->df", normed_low, grad_inner, preferred_element_type=jnp.float32)
    grad_up_bias = jnp.sum(grad_inner.astype(jnp.float32), 0)
    grad_normed = grad_summed + jnp.einsum(
        "nf,df->nd", grad_inner, back_up, preferred_element_type=jnp.float32
    )
    grad_hidden, grad_gain_one, grad_shift_one = norm_back(
        grad_normed, normed_one, inv_std_one, back_gain_one
    )
    grad_branch_attn = grad_hidden.astype(jnp.bfloat16)
    grad_out = jnp.einsum("nd,ne->de", mixed, grad_branch_attn, preferred_element_type=jnp.float32)
    grad_out_bias = jnp.sum(grad_branch_attn.astype(jnp.float32), 0)
    grad_mixed = jnp.einsum(
        "ne,de->nd", grad_branch_attn, back_out, preferred_element_type=jnp.float32
    ).astype(jnp.bfloat16)
    grad_mixed = grad_mixed.reshape(seq_count, length, HEADS, HEAD_DIM)
    grad_projected = lax.map(
        lambda seq_data: attend_backward(*seq_data),
        (queries, keys_all, values_all, grad_mixed, log_total, segment_ids),
    )
    grad_projected = grad_projected.reshape(tokens, 3 * width)
    grad_qkv = jnp.einsum(
        "nd,ne->de", inputs_flat, grad_projected, preferred_element_type=jnp.float32
    )
    grad_bias_all = jnp.sum(grad_projected.astype(jnp.float32), 0)
    grad_query_bias = grad_bias_all[:width]
    grad_value_bias = grad_bias_all[2 * width :]
    input_grad = grad_hidden + jnp.einsum(
        "ne,de->nd", grad_projected, back_qkv, preferred_element_type=jnp.float32
    )
    input_grad = input_grad.astype(jnp.bfloat16).reshape(seq_count, length, width)
    grads = (
        grad_qkv,
        grad_query_bias,
        grad_value_bias,
        grad_out,
        grad_out_bias,
        grad_gain_one,
        grad_shift_one,
        grad_up,
        grad_up_bias,
        grad_down,
        grad_down_bias,
        grad_gain_two,
        grad_shift_two,
    )
    owned = (
        lax.psum_scatter(
            grads[0].astype(jnp.bfloat16), "shard", scatter_dimension=0, tiled=True
        ).astype(jnp.float32),
        lax.psum_scatter(
            grads[1].astype(jnp.bfloat16), "shard", scatter_dimension=0, tiled=True
        ).astype(jnp.float32),
        lax.psum_scatter(
            grads[2].astype(jnp.bfloat16), "shard", scatter_dimension=0, tiled=True
        ).astype(jnp.float32),
        lax.psum_scatter(
            grads[3].astype(jnp.bfloat16), "shard", scatter_dimension=0, tiled=True
        ).astype(jnp.float32),
        lax.psum_scatter(
            grads[4].astype(jnp.bfloat16), "shard", scatter_dimension=0, tiled=True
        ).astype(jnp.float32),
        lax.psum_scatter(
            grads[5].astype(jnp.bfloat16), "shard", scatter_dimension=0, tiled=True
        ).astype(jnp.float32),
        lax.psum_scatter(
            grads[6].astype(jnp.bfloat16), "shard", scatter_dimension=0, tiled=True
        ).astype(jnp.float32),
        lax.psum_scatter(
            grads[7].astype(jnp.bfloat16), "shard", scatter_dimension=0, tiled=True
        ).astype(jnp.float32),
        lax.psum_scatter(
            grads[8].astype(jnp.bfloat16), "shard", scatter_dimension=0, tiled=True
        ).astype(jnp.float32),
        lax.psum_scatter(
            grads[9].astype(jnp.bfloat16), "shard", scatter_dimension=0, tiled=True
        ).astype(jnp.float32),
        lax.psum_scatter(
            grads[10].astype(jnp.bfloat16), "shard", scatter_dimension=0, tiled=True
        ).astype(jnp.float32),
        lax.psum_scatter(
            grads[11].astype(jnp.bfloat16), "shard", scatter_dimension=0, tiled=True
        ).astype(jnp.float32),
        lax.psum_scatter(
            grads[12].astype(jnp.bfloat16), "shard", scatter_dimension=0, tiled=True
        ).astype(jnp.float32),
    )
    summed_grads = (
        lax.psum(owned[0].astype(jnp.bfloat16), "rep").astype(jnp.float32),
        lax.psum(owned[1].astype(jnp.bfloat16), "rep").astype(jnp.float32),
        lax.psum(owned[2].astype(jnp.bfloat16), "rep").astype(jnp.float32),
        lax.psum(owned[3].astype(jnp.bfloat16), "rep").astype(jnp.float32),
        lax.psum(owned[4].astype(jnp.bfloat16), "rep").astype(jnp.float32),
        lax.psum(owned[5].astype(jnp.bfloat16), "rep").astype(jnp.float32),
        lax.psum(owned[6].astype(jnp.bfloat16), "rep").astype(jnp.float32),
        lax.psum(owned[7].astype(jnp.bfloat16), "rep").astype(jnp.float32),
        lax.psum(owned[8].astype(jnp.bfloat16), "rep").astype(jnp.float32),
        lax.psum(owned[9].astype(jnp.bfloat16), "rep").astype(jnp.float32),
        lax.psum(owned[10].astype(jnp.bfloat16), "rep").astype(jnp.float32),
        lax.psum(owned[11].astype(jnp.bfloat16), "rep").astype(jnp.float32),
        lax.psum(owned[12].astype(jnp.bfloat16), "rep").astype(jnp.float32),
    )
    return (layer_output, input_grad) + tuple(summed_grads)


def solution(mesh):
    return jax.shard_map(
        body,
        mesh=mesh,
        in_specs=(
            P(("rep", "shard"), None, None),
            P(("rep", "shard"), None),
            P(("rep", "shard"), None, None),
            P("shard", None),
            P("shard"),
            P("shard"),
            P("shard", None),
            P("shard"),
            P("shard"),
            P("shard"),
            P("shard", None),
            P("shard"),
            P("shard", None),
            P("shard"),
            P("shard"),
            P("shard"),
        ),
        out_specs=(
            P(("rep", "shard"), None, None),
            P(("rep", "shard"), None, None),
            P("shard", None),
            P("shard"),
            P("shard"),
            P("shard", None),
            P("shard"),
            P("shard"),
            P("shard"),
            P("shard", None),
            P("shard"),
            P("shard", None),
            P("shard"),
            P("shard"),
            P("shard"),
        ),
        check_vma=False,
    )
```

profile of v0, /device:TPU:0, one launch (start us, length us, event | category | flops | bytes accessed | tf_op | source)
XLA Modules:
  0.0 709.4 jit_solution(9201289987859553486)
XLA Ops:
  18.6 31.7 %all-reduce.18 = (bf16[768]{0:T(1024)(128)(2,1)S(1)}, bf16[768]{0:T(1024)(128)(2,1)S(1)}, bf16[768]{0:T(1024)(128)(2,1)S(1)}, bf16[768]{0:T(1024)(128)(2,1)S(1)}...) all-reduce(bf16[768]{0:T(1024)(128)(2,1)S(1)} %dynamic-update-slice, ...), channel_id=1, replica_groups=mesh['rep'=4,'shard'=8] {'shard'}, use_global_device_ids=true, to_apply=%add.1 | all-reduce | flops 5376 | bytes 21504
  55.1 12.8 %all-gather = bf16[8,1,384]{2,1,0:T(2,128)(2,1)S(1)} all-gather(bf16[1,1,384]{2,1,0:T(2,128)(2,1)S(1)} %reshape.265), channel_id=1, replica_groups=mesh['rep'=4,'shard'=8] {'shard'}, dimensions={0}, use_global_device_ids=true | all-gather | bytes 6912 | tf_op jit(solution)/shard_map/all_gather | solution.py:155
  72.9 7.5 %add_convert_fusion = bf16[1024,2304]{1,0:T(8,128)(2,1)} fusion(bf16[768,2304]{1,0:T(8,128)(2,1)} %all-gather.6.cloned.1.call-done, f32[2304]{0:T(1024)S(1)} %pad_maximum_fusion.1, bf16[1,1024,768]{2,1,0:T(8,128)(2,1)S(1)} %copy-done.19), kind=kOutput, calls=%fused_computation.55 | convolution fusion | flops 3628597248 | bytes 9839616 | tf_op jit(solution)/shard_map/dot_general | solution.py:184
  80.4 6.8 copy.58
  87.2 4.6 slice_bitcast_fusion
  95.9 71.6 %while.45 = (s32[]{:T(128)}, bf16[2,512,12,64]{1,3,2,0:T(8,128)(2,1)}, f32[2,12,512]{2,1,0:T(8,128)S(1)}, s32[2,512]{1,0:T(2,128)S(1)}, s32[1024]{0:T(1024)S(1)}...) while((s32[]{:T(128)}, ...), condition=%wide.region_3.4_spmd, body=%wide.region_0.3_spmd.sunk | while | flops 1687021568 | bytes 189499568 | solution.py:62
  96.3 10.8 %fusion.103 = (f32[12,512]{1,0:T(8,128)S(1)}, f32[12,512,1024]{2,1,0:T(8,128)}) fusion(pred[512,1024]{1,0:T(8,128)(4,1)S(1)} %broadcast_compare_fusion.4, bf16[1024,12,64]{0,2,1:T(8,128)(2,1)S(1)} %get-tuple-element.546, bf16[2,512,12,64]{1,3,2,0:T(8,128)(2,1)S(1)} %get-tuple-element.545, s32[]{:T(128)S(6)} %copy.92), kind=kOutput, calls=%fused_computation.3.clone.1 | convolution fusion | flops 824174592 | bytes 28073988 | tf_op jit(solution)/shard_map/while/body/eval_jaxpr/while/body/eval_jaxpr/qhd,khd->hqk/dot_general | solution.py:41
  107.1 12.6 %fusion.104 = f32[12,512]{1,0:T(8,128)S(1)} fusion(f32[12,512,1024]{2,1,0:T(8,128)} %get-tuple-element.507, f32[12,512]{1,0:T(8,128)S(1)} %get-tuple-element.508, pred[512,1024]{1,0:T(8,128)(4,1)S(1)} %broadcast_compare_fusion.4), kind=kLoop, calls=%fused_computation.4.clone.1 | loop fusion | flops 25159680 | bytes 25739264 | tf_op jit(solution)/shard_map/while/body/eval_jaxpr/while/body/eval_jaxpr/reduce_sum | solution.py:57
  119.7 3.2 copy-done
  122.9 8.5 %fusion.105 = bf16[2,512,12,64]{1,3,2,0:T(8,128)(2,1)} fusion(bf16[2,512,12,64]{1,3,2,0:T(8,128)(2,1)} %get-tuple-element.532, s32[]{:T(128)S(6)} %copy.92, bf16[1024,12,64]{0,2,1:T(8,128)(2,1)S(1)} %copy-done.4, f32[12,512,1024]{2,1,0:T(8,128)S(1)} %copy-done, f32[12,512]{1,0:T(8,128)S(1)} %fusion.104, f32[12,512]{1,0:T(8,128)S(1)} %get-tuple-element.508, ...), kind=kOutput, calls=%fused_computation.8.clone.1 | convolution fusion | flops 837156864 | bytes 28098564 | tf_op jit(solution)/shard_map/while/body/eval_jaxpr/while/body/eval_jaxpr/hqk,khd->qhd/dot_general | solution.py:59
  131.8 11.1 %fusion.103 = (f32[12,512]{1,0:T(8,128)S(1)}, f32[12,512,1024]{2,1,0:T(8,128)}) fusion(pred[512,1024]{1,0:T(8,128)(4,1)S(1)} %broadcast_compare_fusion.4, bf16[1024,12,64]{0,2,1:T(8,128)(2,1)S(1)} %get-tuple-element.546, bf16[2,512,12,64]{1,3,2,0:T(8,128)(2,1)S(1)} %get-tuple-element.545, s32[]{:T(128)S(6)} %copy.92), kind=kOutput, calls=%fused_computation.3.clone.1 | convolution fusion | flops 824174592 | bytes 28073988 | tf_op jit(solution)/shard_map/while/body/eval_jaxpr/while/body/eval_jaxpr/qhd,khd->hqk/dot_general | solution.py:41
  142.9 12.4 %fusion.104 = f32[12,512]{1,0:T(8,128)S(1)} fusion(f32[12,512,1024]{2,1,0:T(8,128)} %get-tuple-element.507, f32[12,512]{1,0:T(8,128)S(1)} %get-tuple-element.508, pred[512,1024]{1,0:T(8,128)(4,1)S(1)} %broadcast_compare_fusion.4), kind=kLoop, calls=%fused_computation.4.clone.1 | loop fusion | flops 25159680 | bytes 25739264 | tf_op jit(solution)/shard_map/while/body/eval_jaxpr/while/body/eval_jaxpr/reduce_sum | solution.py:57
  155.4 3.4 copy-done
  158.8 8.5 %fusion.105 = bf16[2,512,12,64]{1,3,2,0:T(8,128)(2,1)} fusion(bf16[2,512,12,64]{1,3,2,0:T(8,128)(2,1)} %get-tuple-element.532, s32[]{:T(128)S(6)} %copy.92, bf16[1024,12,64]{0,2,1:T(8,128)(2,1)S(1)} %copy-done.4, f32[12,512,1024]{2,1,0:T(8,128)S(1)} %copy-done, f32[12,512]{1,0:T(8,128)S(1)} %fusion.104, f32[12,512]{1,0:T(8,128)S(1)} %get-tuple-element.508, ...), kind=kOutput, calls=%fused_computation.8.clone.1 | convolution fusion | flops 837156864 | bytes 28098564 | tf_op jit(solution)/shard_map/while/body/eval_jaxpr/while/body/eval_jaxpr/hqk,khd->qhd/dot_general | solution.py:59
  167.5 3.0 copy.60
  172.1 3.9 fusion.60
  178.2 13.7 %multiply_convert_fusion.1 = (bf16[1024,3072]{1,0:T(8,128)(2,1)}, f32[1024,3072]{1,0:T(8,128)}) fusion(f32[3072]{0:T(1024)S(1)} %bitcast.170, bf16[768,3072]{1,0:T(8,128)(2,1)} %all-gather.10.cloned.1.call-done, f32[1024,768]{0,1:T(8,128)} %copy-done.9, f32[768]{0:T(1024)S(1)} %copy-done.41, f32[768]{0:T(1024)S(1)} %copy-done.32, ...), kind=kOutput, calls=%fused_computation.53 | convolution fusion | flops 4854644736 | bytes 26765312 | tf_op jit(solution)/shard_map/dot_general | solution.py:203
  191.9 9.9 %fusion.61 = (f32[1024]{0:T(1024)S(1)}, f32[1024,768]{0,1:T(8,128)S(1)}) fusion(f32[768]{0:T(1024)S(1)} %copy-done.43, bf16[1024,3072]{1,0:T(8,128)(2,1)} %get-tuple-element.389, bf16[3072,768]{1,0:T(8,128)(2,1)} %all-gather.12.cloned.1.call-done, f32[768]{0:T(1024)S(1)} %copy-done.41, f32[768]{0:T(1024)S(1)} %copy-done.32, f32[1024]{0:T(1024)S(1)} %add_rsqrt_fusion.1, ...), kind=kOutput, calls=%fused_computation.110 | convolution fusion | flops 4838915072 | bytes 17323008 | tf_op jit(solution)/shard_map/dot_general | solution.py:209
  208.3 14.7 %fusion.62 = (bf16[3072]{0:T(1024)(128)(2,1)}, bf16[1024,3072]{1,0:T(8,128)(2,1)}) fusion(f32[1024,3072]{1,0:T(8,128)} %get-tuple-element.390, f32[3072]{0:T(1024)S(1)} %bitcast.171, bf16[1024,768]{0,1:T(8,128)(2,1)S(1)} %get-tuple-element.373, bf16[3072,768]{1,0:T(8,128)(2,1)S(1)} %bitcast.175), kind=kOutput, calls=%fused_computation.111 | convolution fusion | flops 4869583872 | bytes 25184256 | tf_op jit(solution)/shard_map/nd,fd->nf/dot_general | solution.py:246
  223.0 9.7 %multiply_reduce_fusion.1 = (bf16[768]{0:T(1024)(128)(2,1)}, f32[1024]{0:T(1024)S(1)}, f32[1024]{0:T(1024)S(1)}, bf16[768]{0:T(1024)(128)(2,1)}, f32[1024,768]{0,1:T(8,128)S(1)}) fusion(f32[1024,768]{0,1:T(8,128)S(1)} %copy-done.10, f32[1024]{0:T(1024)S(1)} %add_rsqrt_fusion.1, f32[1024]{0:T(1024)S(1)} %broadcast_multiply_fusion.5, f32[768]{0:T(1024)S(1)} %copy-done.32, ...), kind=kOutput, calls=%fused_computation.70 | convolution fusion | flops 4845989888 | bytes 22062080 | tf_op jit(solution)/shard_map/nf,df->nd/dot_general | solution.py:252
  241.3 3.8 reshape.235
  248.1 169.8 %while.46 = (s32[]{:T(128)}, f32[1024,12,64]{0,2,1:T(8,128)}, f32[1024,12,64]{0,2,1:T(8,128)}, bf16[2,512,12,64]{1,3,2,0:T(8,128)(2,1)}, bf16[2,512,12,64]{1,3,2...) while((s32[]{:T(128)}, f32[1024,12,64]{0,2,1:T(8,128)}, ...), condition=%wide.region_14.15_spmd.clone, body=%wide.region_12.14_spmd.clone.sunk | while | flops 4125747200 | bytes 231926000 | solution.py:107
  249.8 11.4 %fusion.115 = f32[12,512,1024]{2,1,0:T(8,128)} fusion(bf16[1024,12,64]{0,2,1:T(8,128)(2,1)S(1)} %get-tuple-element.582, bf16[2,512,12,64]{1,3,2,0:T(8,128)(2,1)} %copy-done.2, s32[]{:T(128)S(6)} %copy.103), kind=kOutput, calls=%fused_computation.32.clone.1 | convolution fusion | flops 805306368 | bytes 27525124 | tf_op jit(solution)/shard_map/while/body/eval_jaxpr/while/body/eval_jaxpr/qhd,khd->hqk/dot_general | solution.py:41
  261.2 13.4 %bitcast_add_fusion.5 = f32[1024,12,64]{0,2,1:T(8,128)} fusion(f32[1024,12,64]{0,2,1:T(8,128)} %get-tuple-element.564, f32[12,512,1024]{2,1,0:T(8,128)} %fusion.115, f32[12,512]{1,0:T(8,128)S(1)} %dynamic-slice_bitcast_fusion.2, pred[512,1024]{1,0:T(8,128)(4,1)S(1)} %broadcast_compare_fusion.5, pred[]{:T(512)S(6)} %compare.3, ...), kind=kOutput, calls=%fused_computation.24.clone.1 | convolution fusion | flops 832045056 | bytes 32800772 | tf_op jit(solution)/shard_map/while/body/eval_jaxpr/while/body/eval_jaxpr/hqk,qhd->khd/dot_general | solution.py:82
  274.6 18.1 %multiply_reduce_fusion.7 = (f32[12,512]{1,0:T(8,128)S(1)}, f32[12,512,1024]{2,1,0:T(8,128)}) fusion(f32[12,512,1024]{2,1,0:T(8,128)} %fusion.115, f32[12,512]{1,0:T(8,128)S(1)} %dynamic-slice_bitcast_fusion.2, pred[512,1024]{1,0:T(8,128)(4,1)S(1)} %broadcast_compare_fusion.5, bf16[1024,12,64]{0,2,1:T(8,128)(2,1)} %get-tuple-element.585, ...), kind=kOutput, calls=%fused_computation.19.clone.1 | convolution fusion | flops 836757504 | bytes 53264388 | tf_op jit(solution)/shard_map/while/body/eval_jaxpr/while/body/eval_jaxpr/qhd,khd->hqk/dot_general | solution.py:88
  292.7 21.2 %multiply_convert_fusion.3 = bf16[12,512,1024]{2,1,0:T(8,128)(2,1)} fusion(f32[12,512,1024]{2,1,0:T(8,128)} %get-tuple-element.520, f32[12,512,1024]{2,1,0:T(8,128)} %fusion.115, f32[12,512]{1,0:T(8,128)S(1)} %get-tuple-element.521, f32[12,512]{1,0:T(8,128)S(1)} %dynamic-slice_bitcast_fusion.2, pred[512,1024]{1,0:T(8,128)(4,1)S(1)} %broadcast_compare_fusion.5), kind=kLoop, calls=%fused_computation.18.clone.1 | loop fusion | flops 37748736 | bytes 63488000 | tf_op jit(solution)/shard_map/while/body/eval_jaxpr/while/body/eval_jaxpr/convert_element_type | solution.py:92
  314.0 9.6 %bitcast_dynamic-update-slice_fusion.5 = bf16[2,512,12,64]{1,3,2,0:T(8,128)(2,1)} fusion(bf16[2,512,12,64]{1,3,2,0:T(8,128)(2,1)} %get-tuple-element.565, s32[]{:T(128)S(6)} %copy.103, bf16[12,512,1024]{2,1,0:T(8,128)(2,1)} %multiply_convert_fusion.3, bf16[1024,12,64]{0,2,1:T(8,128)(2,1)S(1)} %get-tuple-element.582), kind=kOutput, calls=%fused_computation.26.clone.1 | convolution fusion | flops 805699584 | bytes 15728644 | tf_op jit(solution)/shard_map/while/body/eval_jaxpr/while/body/eval_jaxpr/hqk,khd->qhd/dot_general | solution.py:94
  323.6 8.5 %bitcast_add_fusion.4 = f32[1024,12,64]{0,2,1:T(8,128)} fusion(f32[1024,12,64]{0,2,1:T(8,128)} %get-tuple-element.563, bf16[12,512,1024]{2,1,0:T(8,128)(2,1)} %multiply_convert_fusion.3, pred[]{:T(512)S(6)} %compare.3, bf16[2,512,12,64]{1,3,2,0:T(8,128)(2,1)S(1)} %copy-done.3, s32[]{:T(128)S(6)} %copy.103), kind=kOutput, calls=%fused_computation.25.clone.1 | convolution fusion | flops 807665664 | bytes 19660804 | tf_op jit(solution)/shard_map/while/body/eval_jaxpr/while/body/eval_jaxpr/hqk,qhd->khd/dot_general | solution.py:99
  333.7 11.4 %fusion.115 = f32[12,512,1024]{2,1,0:T(8,128)} fusion(bf16[1024,12,64]{0,2,1:T(8,128)(2,1)S(1)} %get-tuple-element.582, bf16[2,512,12,64]{1,3,2,0:T(8,128)(2,1)} %copy-done.2, s32[]{:T(128)S(6)} %copy.103), kind=kOutput, calls=%fused_computation.32.clone.1 | convolution fusion | flops 805306368 | bytes 27525124 | tf_op jit(solution)/shard_map/while/body/eval_jaxpr/while/body/eval_jaxpr/qhd,khd->hqk/dot_general | solution.py:41
  345.1 14.3 %bitcast_add_fusion.5 = f32[1024,12,64]{0,2,1:T(8,128)} fusion(f32[1024,12,64]{0,2,1:T(8,128)} %get-tuple-element.564, f32[12,512,1024]{2,1,0:T(8,128)} %fusion.115, f32[12,512]{1,0:T(8,128)S(1)} %dynamic-slice_bitcast_fusion.2, pred[512,1024]{1,0:T(8,128)(4,1)S(1)} %broadcast_compare_fusion.5, pred[]{:T(512)S(6)} %compare.3, ...), kind=kOutput, calls=%fused_computation.24.clone.1 | convolution fusion | flops 832045056 | bytes 32800772 | tf_op jit(solution)/shard_map/while/body/eval_jaxpr/while/body/eval_jaxpr/hqk,qhd->khd/dot_general | solution.py:82
  359.4 18.1 %multiply_reduce_fusion.7 = (f32[12,512]{1,0:T(8,128)S(1)}, f32[12,512,1024]{2,1,0:T(8,128)}) fusion(f32[12,512,1024]{2,1,0:T(8,128)} %fusion.115, f32[12,512]{1,0:T(8,128)S(1)} %dynamic-slice_bitcast_fusion.2, pred[512,1024]{1,0:T(8,128)(4,1)S(1)} %broadcast_compare_fusion.5, bf16[1024,12,64]{0,2,1:T(8,128)(2,1)} %get-tuple-element.585, ...), kind=kOutput, calls=%fused_computation.19.clone.1 | convolution fusion | flops 836757504 | bytes 53264388 | tf_op jit(solution)/shard_map/while/body/eval_jaxpr/while/body/eval_jaxpr/qhd,khd->hqk/dot_general | solution.py:88
  377.5 21.2 %multiply_convert_fusion.3 = bf16[12,512,1024]{2,1,0:T(8,128)(2,1)} fusion(f32[12,512,1024]{2,1,0:T(8,128)} %get-tuple-element.520, f32[12,512,1024]{2,1,0:T(8,128)} %fusion.115, f32[12,512]{1,0:T(8,128)S(1)} %get-tuple-element.521, f32[12,512]{1,0:T(8,128)S(1)} %dynamic-slice_bitcast_fusion.2, pred[512,1024]{1,0:T(8,128)(4,1)S(1)} %broadcast_compare_fusion.5), kind=kLoop, calls=%fused_computation.18.clone.1 | loop fusion | flops 37748736 | bytes 63488000 | tf_op jit(solution)/shard_map/while/body/eval_jaxpr/while/body/eval_jaxpr/convert_element_type | solution.py:92
  398.8 9.5 %bitcast_dynamic-update-slice_fusion.5 = bf16[2,512,12,64]{1,3,2,0:T(8,128)(2,1)} fusion(bf16[2,512,12,64]{1,3,2,0:T(8,128)(2,1)} %get-tuple-element.565, s32[]{:T(128)S(6)} %copy.103, bf16[12,512,1024]{2,1,0:T(8,128)(2,1)} %multiply_convert_fusion.3, bf16[1024,12,64]{0,2,1:T(8,128)(2,1)S(1)} %get-tuple-element.582), kind=kOutput, calls=%fused_computation.26.clone.1 | convolution fusion | flops 805699584 | bytes 15728644 | tf_op jit(solution)/shard_map/while/body/eval_jaxpr/while/body/eval_jaxpr/hqk,khd->qhd/dot_general | solution.py:94
  408.3 9.4 %bitcast_add_fusion.4 = f32[1024,12,64]{0,2,1:T(8,128)} fusion(f32[1024,12,64]{0,2,1:T(8,128)} %get-tuple-element.563, bf16[12,512,1024]{2,1,0:T(8,128)(2,1)} %multiply_convert_fusion.3, pred[]{:T(512)S(6)} %compare.3, bf16[2,512,12,64]{1,3,2,0:T(8,128)(2,1)S(1)} %copy-done.3, s32[]{:T(128)S(6)} %copy.103), kind=kOutput, calls=%fused_computation.25.clone.1 | convolution fusion | flops 807665664 | bytes 19660804 | tf_op jit(solution)/shard_map/while/body/eval_jaxpr/while/body/eval_jaxpr/hqk,qhd->khd/dot_general | solution.py:99
  417.9 3.2 copy.67
  426.0 7.3 %fusion.40 = bf16[768,2304]{0,1:T(8,128)(2,1)S(1)} fusion(bf16[1,1024,768]{2,1,0:T(8,128)(2,1)S(1)} %copy-done.20, bf16[1024,768]{0,1:T(8,128)(2,1)S(1)} %bitcast.160, bf16[1024,768]{0,1:T(8,128)(2,1)S(1)} %bitcast.157, bf16[1024,768]{0,1:T(8,128)(2,1)S(1)} %bitcast.154), kind=kOutput, calls=%fused_computation.60 | convolution fusion | flops 3639803904 | bytes 9830400 | tf_op jit(solution)/shard_map/nd,ne->de/dot_general | solution.py:270
  433.3 4.0 copy.75
  439.3 3.8 convolution_convert_fusion.4
  443.2 9.2 %convolution_convert_fusion = bf16[3072,768]{1,0:T(8,128)(2,1)} fusion(bf16[1024,3072]{1,0:T(8,128)(2,1)} %get-tuple-element.389, bf16[1024,768]{0,1:T(8,128)(2,1)} %copy-done.21), kind=kOutput, calls=%fused_computation.56 | convolution fusion | flops 4834197504 | bytes 12582912 | tf_op jit(solution)/shard_map/nf,nd->fd/dot_general | solution.py:242
  454.3 10.2 %convolution_convert_fusion.1 = bf16[768,3072]{1,0:T(8,128)(2,1)} fusion(bf16[1024,3072]{1,0:T(8,128)(2,1)} %get-tuple-element.395, f32[1024,768]{0,1:T(8,128)S(1)} %copy-done.11, f32[768]{0:T(1024)S(1)} %copy-done.42, f32[768]{0:T(1024)S(1)} %copy-done.33, f32[1024]{0:T(1024)S(1)} %copy-done.35, f32[1024]{0:T(1024)S(1)} %copy-done.31), kind=kOutput, calls=%fused_computation.57 | convolution fusion | flops 4838129664 | bytes 14170112 | tf_op jit(solution)/shard_map/nd,nf->df/dot_general | solution.py:250
  466.6 12.8 %reduce-scatter.13.cloned.1.call-done = bf16[96,2304]{1,0:T(8,128)(2,1)} async-done(((bf16[768,2304]{1,0:T(8,128)(2,1)}), bf16[96,2304]{1,0:T(8,128)(2,1)}) %reduce-scatter.13.cloned.1.call-update) | async-done | bytes 442384
  481.5 31.9 %reduce-scatter.7.cloned.1.call-done = bf16[96,768]{1,0:T(8,128)(2,1)} async-done(((bf16[768,768]{1,0:T(8,128)(2,1)}), bf16[96,768]{1,0:T(8,128)(2,1)}) %reduce-scatter.7.cloned.1.call-update) | async-done | bytes 147472 | tf_op jit(solution)/shard_map/reduce_scatter | solution.py:305
  513.4 55.8 %reduce-scatter.11.cloned.1.call-done = bf16[384,768]{1,0:T(8,128)(2,1)} async-done(((bf16[3072,768]{1,0:T(8,128)(2,1)}), bf16[384,768]{1,0:T(8,128)(2,1)}) %reduce-scatter.11.cloned.1.call-update) | async-done | bytes 589840 | tf_op jit(solution)/shard_map/reduce_scatter | solution.py:323
  569.2 55.8 %reduce-scatter.9.cloned.1.call-done = bf16[96,3072]{1,0:T(8,128)(2,1)} async-done(((bf16[768,3072]{1,0:T(8,128)(2,1)}), bf16[96,3072]{1,0:T(8,128)(2,1)}) %reduce-scatter.9.cloned.1.call-update) | async-done | bytes 589840 | tf_op jit(solution)/shard_map/reduce_scatter | solution.py:317
  625.0 7.7 %fusion.51 = bf16[1,1024,768]{1,2,0:T(8,128)(2,1)S(1)} fusion(f32[1024,768]{0,1:T(8,128)} %copy-done.17, bf16[768,2304]{1,0:T(8,128)(2,1)} %all-gather.6.cloned.1.call-done, bf16[1024,768]{0,1:T(8,128)(2,1)} %bitcast.161, bf16[1024,768]{0,1:T(8,128)(2,1)} %bitcast.158, bf16[1024,768]{0,1:T(8,128)(2,1)S(1)} %bitcast.156), kind=kOutput, calls=%fused_computation.91 | convolution fusion | flops 3639607296 | bytes 12976128 | tf_op jit(solution)/shard_map/ne,de->nd/dot_general | solution.py:276
  637.3 26.0 %all-reduce.17 = (bf16[768]{0:T(1024)(128)(2,1)S(1)}, bf16[768]{0:T(1024)(128)(2,1)S(1)}, bf16[768]{0:T(1024)(128)(2,1)S(1)}, bf16[768]{0:T(1024)(128)(2,1)S(1)}...) all-reduce(bf16[768]{0:T(1024)(128)(2,1)S(1)} %dynamic-update-slice, ...), channel_id=1, replica_groups=mesh['rep'=4,'shard'=8] {'shard'}, use_global_device_ids=true, to_apply=%add.7 | all-reduce | flops 9984 | bytes 39936
  663.9 10.4 %all-reduce.19 = (bf16[96]{0:T(256)(128)(2,1)S(1)}, bf16[96]{0:T(256)(128)(2,1)S(1)}, bf16[96]{0:T(256)(128)(2,1)S(1)}, bf16[96]{0:T(256)(128)(2,1)S(1)}, bf16[9...) all-reduce(bf16[96]{0:T(256)(128)(2,1)S(1)} %dynamic-slice.10, ...), channel_id=1, replica_groups=mesh['rep'=4,'shard'=8] {'rep'}, use_global_device_ids=true, to_apply=%region_19.20 | all-reduce | flops 1152 | bytes 4608 | tf_op jit(solution)/shard_map/psum | solution.py:338
  683.3 11.9 %all-reduce.23.cloned.1.call-done = (bf16[96,2304]{0,1:T(8,128)(2,1)}, bf16[96,768]{1,0:T(8,128)(2,1)}, bf16[96,3072]{1,0:T(8,128)(2,1)}, bf16[384,768]{1,0:T(8,128)(2,1)}) async-done(((bf16[96,2304]{0,1:T(8,128)(2,1)}, bf16[96,768]{1,0:T(8,128)(2,1)}, bf16[96,3072]{1,0:T(8,128)(2,1)}, bf16[384,768]{1,0:T(8,128)(2,1)}), (bf16[96,2304]{0,1:T(8,128)(2,1)}, bf16[96,768]{1,0:T(8,128)(2,1)}, ...) | async-done | bytes 1769488 | tf_op jit(solution)/shard_map/psum | solution.py:337
  (239 shorter events, 82.6 us)
Async XLA Ops:
  7.2 64.0 %copy-start.19 = (bf16[1,1024,768]{2,1,0:T(8,128)(2,1)S(1)}, bf16[1,1024,768]{2,1,0:T(8,128)(2,1)}, u32[]{:S(2)}) copy-start(bf16[1,1024,768]{2,1,0:T(8,128)(2,1)} %param.20) | copy-start | bytes 4718596
  7.2 65.7 %all-gather.6.cloned.1.call-start = ((), (), s32[]{:S(2)}) async-start(), calls=%async_computation.4 | async-start | bytes 3981312 | tf_op jit(solution)/shard_map/all_gather | solution.py:147
  7.9 164.2 %all-gather.8.cloned.1.call-start = ((), (), s32[]{:S(2)}) async-start(), calls=%async_computation.5 | async-start | bytes 1327104 | tf_op jit(solution)/shard_map/all_gather | solution.py:150
  8.7 169.5 %all-gather.10.cloned.1.call-start = ((), (), s32[]{:S(2)}) async-start(), calls=%async_computation.6 | async-start | bytes 5308416 | tf_op jit(solution)/shard_map/all_gather | solution.py:154
  9.4 182.5 %all-gather.12.cloned.1.call-start = ((), (), s32[]{:S(2)}) async-start(), calls=%async_computation.7 | async-start | bytes 5308416 | tf_op jit(solution)/shard_map/all_gather | solution.py:156
  10.0 469.5 %reduce-scatter.13.cloned.1.call-start = ((), (), s32[]{:S(2)}) async-start(), calls=%async_computation.11 | async-start | bytes 3981312
  91.8 4.1 copy-start.23
  96.3 23.4 %copy-start.4 = (bf16[1024,12,64]{0,2,1:T(8,128)(2,1)S(1)}, bf16[1024,12,64]{0,2,1:T(8,128)(2,1)}, u32[]{:S(2)}) copy-start(bf16[1024,12,64]{0,2,1:T(8,128)(2,1)} %get-tuple-element.547) | copy-start | bytes 4718596 | tf_op jit(solution)/shard_map/while/body/eval_jaxpr/while
  107.1 15.8 %copy-start = (f32[12,512,1024]{2,1,0:T(8,128)S(1)}, f32[12,512,1024]{2,1,0:T(8,128)}, u32[]{:S(2)}) copy-start(f32[12,512,1024]{2,1,0:T(8,128)} %get-tuple-element.507) | copy-start | bytes 75497472 | tf_op jit(solution)/shard_map/while/body/eval_jaxpr/while
  131.8 23.5 %copy-start.4 = (bf16[1024,12,64]{0,2,1:T(8,128)(2,1)S(1)}, bf16[1024,12,64]{0,2,1:T(8,128)(2,1)}, u32[]{:S(2)}) copy-start(bf16[1024,12,64]{0,2,1:T(8,128)(2,1)} %get-tuple-element.547) | copy-start | bytes 4718596 | tf_op jit(solution)/shard_map/while/body/eval_jaxpr/while
  142.9 15.8 %copy-start = (f32[12,512,1024]{2,1,0:T(8,128)S(1)}, f32[12,512,1024]{2,1,0:T(8,128)}, u32[]{:S(2)}) copy-start(f32[12,512,1024]{2,1,0:T(8,128)} %get-tuple-element.507) | copy-start | bytes 75497472 | tf_op jit(solution)/shard_map/while/body/eval_jaxpr/while
  167.5 4.6 copy-start.44
  176.1 56.6 %copy-start.30 = (f32[1024]{0:T(1024)}, f32[1024]{0:T(1024)S(1)}, u32[]{:S(2)}) copy-start(f32[1024]{0:T(1024)S(1)} %broadcast_multiply_fusion.5) | copy-start | bytes 12292
  178.1 54.6 %copy-start.34 = (f32[1024]{0:T(1024)}, f32[1024]{0:T(1024)S(1)}, u32[]{:S(2)}) copy-start(f32[1024]{0:T(1024)S(1)} %add_rsqrt_fusion.1) | copy-start | bytes 12292
  178.2 13.7 %copy-start.43 = (f32[768]{0:T(1024)S(1)}, f32[768]{0:T(1024)}, u32[]{:S(2)}) copy-start(f32[768]{0:T(1024)} %convert_element_type.197) | copy-start | bytes 9220
  201.8 21.1 %copy-start.5 = (f32[1024,768]{0,1:T(8,128)}, f32[1024,768]{0,1:T(8,128)S(1)}, u32[]{:S(2)}) copy-start(f32[1024,768]{0,1:T(8,128)S(1)} %get-tuple-element.392) | copy-start | bytes 9437188
  201.9 21.1 %copy-start.24 = (f32[1024]{0:T(1024)}, f32[1024]{0:T(1024)S(1)}, u32[]{:S(2)}) copy-start(f32[1024]{0:T(1024)S(1)} %broadcast_multiply_fusion.4) | copy-start | bytes 12292
  201.9 6.4 slice-start.2
  204.4 18.6 %copy-start.28 = (f32[1024]{0:T(1024)}, f32[1024]{0:T(1024)S(1)}, u32[]{:S(2)}) copy-start(f32[1024]{0:T(1024)S(1)} %add_rsqrt_fusion) | copy-start | bytes 12292
  204.4 3.8 slice-start.3
  206.3 16.6 %slice-start = ((s8[4718592]{0:T(1024)(128)(4,1)}), s8[4194304]{0:T(1024)(128)(4,1)S(1)}, s32[]{:S(2)}) async-start(s8[4718592]{0:T(1024)(128)(4,1)} %bitcast.172), calls=%async_computation.13 | async-start | bytes 8388608
  208.2 14.7 %copy-start.21 = (bf16[1024,768]{0,1:T(8,128)(2,1)}, bf16[1024,768]{0,1:T(8,128)(2,1)S(1)}, u32[]{:S(2)}) copy-start(bf16[1024,768]{0,1:T(8,128)(2,1)S(1)} %get-tuple-element.373) | copy-start | bytes 4718596
  208.2 14.7 %copy-start.10 = (f32[1024,768]{0,1:T(8,128)S(1)}, f32[1024,768]{0,1:T(8,128)}, u32[]{:S(2)}) copy-start(f32[1024,768]{0,1:T(8,128)} %copy-done.9) | copy-start | bytes 9437188
  208.2 14.7 %slice-start.1 = ((s8[4718592]{0:T(1024)(128)(4,1)}), s8[524288]{0:T(1024)(128)(4,1)S(1)}, s32[]{:S(2)}) async-start(s8[4718592]{0:T(1024)(128)(4,1)} %bitcast.172), calls=%async_computation.14 | async-start | bytes 1048576
  232.7 3.4 copy-start.47
  249.8 11.5 %copy-start.7 = (bf16[2,512,12,64]{1,3,2,0:T(8,128)(2,1)S(1)}, bf16[2,512,12,64]{1,3,2,0:T(8,128)(2,1)}, u32[]{:S(2)}) copy-start(bf16[2,512,12,64]{1,3,2,0:T(8,128)(2,1)} %get-tuple-element.584) | copy-start | bytes 4718596 | tf_op jit(solution)/shard_map/while/body/eval_jaxpr/while
  314.0 9.6 %copy-start.3 = (bf16[2,512,12,64]{1,3,2,0:T(8,128)(2,1)S(1)}, bf16[2,512,12,64]{1,3,2,0:T(8,128)(2,1)}, u32[]{:S(2)}) copy-start(bf16[2,512,12,64]{1,3,2,0:T(8,128)(2,1)} %copy-done.2) | copy-start | bytes 4718596 | tf_op jit(solution)/shard_map/while/body/eval_jaxpr/while
  333.7 11.5 %copy-start.7 = (bf16[2,512,12,64]{1,3,2,0:T(8,128)(2,1)S(1)}, bf16[2,512,12,64]{1,3,2,0:T(8,128)(2,1)}, u32[]{:S(2)}) copy-start(bf16[2,512,12,64]{1,3,2,0:T(8,128)(2,1)} %get-tuple-element.584) | copy-start | bytes 4718596 | tf_op jit(solution)/shard_map/while/body/eval_jaxpr/while
  398.8 9.5 %copy-start.3 = (bf16[2,512,12,64]{1,3,2,0:T(8,128)(2,1)S(1)}, bf16[2,512,12,64]{1,3,2,0:T(8,128)(2,1)}, u32[]{:S(2)}) copy-start(bf16[2,512,12,64]{1,3,2,0:T(8,128)(2,1)} %copy-done.2) | copy-start | bytes 4718596 | tf_op jit(solution)/shard_map/while/body/eval_jaxpr/while
  417.9 3.6 copy-start.1
  421.5 3.3 copy-start.13
  421.8 3.1 copy-start.15
  421.8 4.2 copy-start.20
  437.4 76.0 %reduce-scatter.7.cloned.1.call-start = ((), (), s32[]{:S(2)}) async-start(), calls=%async_computation.8 | async-start | bytes 1327104 | tf_op jit(solution)/shard_map/reduce_scatter | solution.py:305
  443.1 126.1 %reduce-scatter.11.cloned.1.call-start = ((), (), s32[]{:S(2)}) async-start(), calls=%async_computation.10 | async-start | bytes 5308416 | tf_op jit(solution)/shard_map/reduce_scatter | solution.py:323
  452.4 172.6 %reduce-scatter.9.cloned.1.call-start = ((), (), s32[]{:S(2)}) async-start(), calls=%async_computation.9 | async-start | bytes 5308416 | tf_op jit(solution)/shard_map/reduce_scatter | solution.py:317
  464.4 160.5 %copy-start.14 = (bf16[96,8,2,512]{3,1,2,0:T(8,128)(2,1)S(1)}, bf16[96,8,2,512]{3,1,2,0:T(8,128)(2,1)}, u32[]{:S(2)}) copy-start(bf16[96,8,2,512]{3,1,2,0:T(8,128)(2,1)} %copy-done.13) | copy-start | bytes 4718596
  464.5 230.8 %all-reduce.23.cloned.1.call-start = ((), (), s32[]{:S(2)}) async-start(), calls=%async_computation.12 | async-start | bytes 3833856 | tf_op jit(solution)/shard_map/psum | solution.py:337
  634.3 3.0 copy-start.38
  634.3 3.0 copy-start.39
  634.3 3.0 copy-start.40
  634.3 3.0 copy-start.45
  634.3 3.0 copy-start.46
  634.3 44.7 %copy-start.6 = (f32[1024,768]{0,1:T(8,128)S(1)}, f32[1024,768]{0,1:T(8,128)}, u32[]{:S(2)}) copy-start(f32[1024,768]{0,1:T(8,128)} %copy-done.5) | copy-start | bytes 9437188
  634.3 44.7 %copy-start.25 = (f32[1024]{0:T(1024)S(1)}, f32[1024]{0:T(1024)}, u32[]{:S(2)}) copy-start(f32[1024]{0:T(1024)} %copy-done.24) | copy-start | bytes 12292
  634.3 44.7 %copy-start.27 = (f32[768]{0:T(1024)S(1)}, f32[768]{0:T(1024)}, u32[]{:S(2)}) copy-start(f32[768]{0:T(1024)} %convert_element_type.198) | copy-start | bytes 9220
  634.3 44.7 %copy-start.29 = (f32[1024]{0:T(1024)S(1)}, f32[1024]{0:T(1024)}, u32[]{:S(2)}) copy-start(f32[1024]{0:T(1024)} %copy-done.28) | copy-start | bytes 12292
  695.3 6.1 copy-start.22
  (19 other events, 36.4 us)
Sparse Core Ops, SparseCore 0:
  9.7 44.9 all-gather.5
  56.3 21.3 all-gather.7
  79.4 51.4 all-gather.9
  132.4 50.5 all-gather.11
  437.5 41.8 reduce-scatter.12
  482.3 31.1 reduce-scatter.6
  515.8 53.3 reduce-scatter.10
  571.6 53.3 reduce-scatter.8
  629.4 65.7 all-reduce.22
where the time goes:
time: 719 us; the launch traced here: 709 us
  matrix products  263 us (37%)
  waiting for transfers between devices  171 us (24%)
  other arithmetic  97.9 us (14%)
  blocking collectives  80.8 us (11%)
  local copies, waits for them, and re-layouts  78.5 us (11%)
  between operations  17.2 us (2%)
    unnamed x2, blocking collectives  57.7 us
    reduce_scatter x1, waiting for transfers between devices, body(): lax.psum_scatter(grads[7].astype(jnp.bfloat16), 'shard', scatter_dimensio...  55.8 us
    reduce_scatter x1, waiting for transfers between devices, body(): lax.psum_scatter(grads[9].astype(jnp.bfloat16), 'shard', scatter_dimensio...  55.8 us
    dot_general x4, matrix products, block_scores(): jnp.einsum('qhd,khd->hqk', query_rows, keys_all, preferred_element_type=j...  44.8 us
    convert_element_type x2, other arithmetic, one_block(): grad_scores = (weights * (grad_weights - row_dot)).astype(jnp.bfloat16)  42.5 us
    unnamed x134, local copies, waits for them, and re-layouts  41.4 us
    dot_general x2, matrix products, one_block(): jnp.einsum('qhd,khd->hqk', grad_rows, values_all, preferred_element_type=...  36.2 us
    reduce_scatter x1, waiting for transfers between devices, body(): lax.psum_scatter(grads[3].astype(jnp.bfloat16), 'shard', scatter_dimensio...  31.9 us
  transfers between devices with their start and end apart: 9, of which 5 were waited for; matrix products, arithmetic and copies ran while one was open for 25% of the time, Pallas kernels for 0%

commit v1 on v0

v1 whole, which is shorter than its diff:
```python
import functools
import math

import jax
import jax.numpy as jnp
from jax import lax
from jax.experimental import pallas as pl
from jax.experimental.pallas import tpu as pltpu
from jax.sharding import PartitionSpec as P

HEAD_DIM = 64
BIG = 2.0**100
BF = jnp.bfloat16
F32 = jnp.float32
NN = (((1,), (0,)), ((), ()))
NT = (((1,), (1,)), ((), ()))
TN = (((0,), (0,)), ((), ()))


def dot(a, b, dims=NN):
    return lax.dot_general(a, b, dims, preferred_element_type=F32)


def tree(op, x):
    while x.shape[0] > 8:
        half = x.shape[0] // 2
        x = op(x[:half], x[half:])
    return x


def split3(x):
    hi = x.astype(BF).astype(F32)
    rest = x - hi
    mid = rest.astype(BF).astype(F32)
    return hi, mid, rest - mid


def doc_features(seg):
    lane = lax.broadcasted_iota(jnp.int32, (seg.shape[0], 128), 1) % 64
    same = seg[:, None] == lane
    query_side = jnp.where(same, 1.0, 0.0).astype(BF)
    key_side = jnp.where(
        lane < 8, jnp.where(same, 0.0, -BIG), jnp.where(lane < 11, 1.0, 0.0)
    ).astype(BF)
    return query_side, key_side


def fwd_kernel(q_ref, k_ref, v_ref, fq_ref, fk_ref, o_ref, fl_ref, kh_s, vt_s, *, bq):
    length = q_ref.shape[0]
    lane = lax.broadcasted_iota(jnp.int32, (length, 128), 1)
    first = lane < 64
    k2 = k_ref[...]
    fk = fk_ref[...]
    kh_s[0] = jnp.where(first, k2, fk)
    kh_s[1] = jnp.where(first, fk, k2)
    vt_s[...] = v_ref[...].T
    firstq = lax.broadcasted_iota(jnp.int32, (bq, 128), 1) < 64
    row = lax.broadcasted_iota(jnp.int32, (128, bq), 0)
    def step(i, carry):
        rows = pl.ds(pl.multiple_of(i * bq, bq), bq)
        q2 = q_ref[rows, :] * BF(0.125)
        fq = fq_ref[rows, :]
        outs, feats = [], []
        for h in range(2):
            qh = jnp.where(firstq, q2, fq) if h == 0 else jnp.where(firstq, fq, q2)
            st = dot(kh_s[h], qh, NT)
            top = jnp.max(tree(jnp.maximum, st), 0, keepdims=True)
            ex = jnp.exp(st - top)
            tot = jnp.sum(tree(jnp.add, ex), 0, keepdims=True)
            ot = dot(vt_s[64 * h:64 * h + 64, :], ex.astype(BF))
            outs.append(ot * (1.0 / tot))
            feats.append(split3(-(top + jnp.log(tot))))
        o_ref[rows, :] = jnp.concatenate(outs, 0).T.astype(BF)
        f = jnp.zeros((128, bq), F32)
        for h in range(2):
            base = 72 if h == 0 else 8
            for j in range(3):
                f = jnp.where(row == base + j, feats[h][j], f)
        fl_ref[rows, :] = f.T.astype(BF) + fq
        return carry
    lax.fori_loop(0, length // bq, step, 0)

def attn_fwd(projected, fq, fk, bq=512):
    length = projected.shape[0]
    width = projected.shape[1] // 3
    nb = width // 128
    blk = lambda off: pl.BlockSpec((length, 128), lambda p: (0, off + p))
    full = pl.BlockSpec((length, 128), lambda p: (0, 0))
    return pl.pallas_call(
        functools.partial(fwd_kernel, bq=bq),
        grid=(nb,),
        in_specs=[blk(0), blk(nb), blk(2 * nb), full, full],
        out_specs=[blk(0), blk(0)],
        out_shape=[jax.ShapeDtypeStruct((length, width), BF)] * 2,
        scratch_shapes=[pltpu.VMEM((2, length, 128), BF), pltpu.VMEM((128, length), BF)],
        compiler_params=pltpu.CompilerParams(vmem_limit_bytes=48 << 20),
        cost_estimate=pl.CostEstimate(flops=4 * nb * 256 * length * length, bytes_accessed=10 * length * width, transcendentals=2 * nb * length * length),
        name="attn_fwd",
    )(projected, projected, projected, fq, fk)

def bwd_kernel(q_ref, k_ref, v_ref, g_ref, o_ref, fl_ref, fk_ref, dq_ref, dk_ref, dv_ref,
               qh_s, gh_s, qs_s, dqt_s, *, bk):
    length = q_ref.shape[0]
    lane = lax.broadcasted_iota(jnp.int32, (length, 128), 1)
    first = lane < 64
    q2 = q_ref[...] * BF(0.125)
    fl = fl_ref[...]
    g2 = g_ref[...]
    qs_s[...] = q2
    qh_s[0] = jnp.where(first, q2, fl)
    qh_s[1] = jnp.where(first, fl, q2)
    prod = g2.astype(F32) * o_ref[...].astype(F32)
    hi = prod.astype(BF)
    lo = (prod - hi.astype(F32)).astype(BF)
    ri = lax.broadcasted_iota(jnp.int32, (128, 128), 0)
    ci = lax.broadcasted_iota(jnp.int32, (128, 128), 1)
    cross = jnp.where((ri < 64) != (ci < 64), -1.0, 0.0).astype(BF)
    neg = dot(hi, cross) + dot(lo, cross)
    a, b, c = split3(neg)
    l64 = lane % 64
    fd = jnp.where(l64 == 8, a, jnp.where(l64 == 9, b, jnp.where(l64 == 10, c, 0.0))).astype(BF)
    gh_s[0] = jnp.where(first, g2, fd)
    gh_s[1] = jnp.where(first, fd, g2)
    dqt_s[...] = jnp.zeros_like(dqt_s)
    firstk = lax.broadcasted_iota(jnp.int32, (bk, 128), 1) < 64
    def step(i, carry):
        rows = pl.ds(pl.multiple_of(i * bk, bk), bk)
        k2 = k_ref[rows, :]
        v2 = v_ref[rows, :]
        fk = fk_ref[rows, :]
        kt = k2.T
        dks, dvs = [], []
        for h in range(2):
            kh = jnp.where(firstk, k2, fk) if h == 0 else jnp.where(firstk, fk, k2)
            vh = jnp.where(firstk, v2, fk) if h == 0 else jnp.where(firstk, fk, v2)
            pt = jnp.exp(dot(kh, qh_s[h], NT))
            dpt = dot(vh, gh_s[h], NT)
            ds = (pt * dpt).astype(BF)
            dvs.append(dot(pt.astype(BF), g_ref[...]))
            dks.append(dot(ds, qs_s[...]))
            dqt_s[64 * h:64 * h + 64, :] += dot(kt[64 * h:64 * h + 64, :], ds)
        dk_ref[rows, :] = jnp.where(firstk, dks[0], dks[1]).astype(BF)
        dv_ref[rows, :] = jnp.where(firstk, dvs[0], dvs[1]).astype(BF)
        return carry
    lax.fori_loop(0, length // bk, step, 0)
    dq_ref[...] = (dqt_s[...] * 0.125).T.astype(BF)

def attn_bwd(projected, grad_mixed, mixed, fl, fk, bk=512, first_pair=0, pairs=None):
    length = projected.shape[0]
    width = projected.shape[1] // 3
    nb = width // 128
    pairs = nb if pairs is None else pairs
    blk = lambda off: pl.BlockSpec((length, 128), lambda p: (0, off + p))
    full = pl.BlockSpec((length, 128), lambda p: (0, 0))
    f = first_pair
    return pl.pallas_call(
        functools.partial(bwd_kernel, bk=bk),
        grid=(pairs,),
        in_specs=[blk(f), blk(nb + f), blk(2 * nb + f), blk(f), blk(f), blk(f), full],
        out_specs=[blk(0), blk(0), blk(0)],
        out_shape=[jax.ShapeDtypeStruct((length, pairs * 128), BF)] * 3,
        scratch_shapes=[pltpu.VMEM((2, length, 128), BF), pltpu.VMEM((2, length, 128), BF),
                        pltpu.VMEM((length, 128), BF), pltpu.VMEM((128, length), F32)],
        compiler_params=pltpu.CompilerParams(vmem_limit_bytes=48 << 20),
        cost_estimate=pl.CostEstimate(flops=10 * pairs * 256 * length * length, bytes_accessed=18 * length * pairs * 128, transcendentals=2 * pairs * length * length),
        name="attn_bwd",
    )(projected, projected, projected, grad_mixed, mixed, fl, fk)


def layer_norm(values, gain, shift):
    centred = values - jnp.mean(values, -1, keepdims=True)
    inv_std = lax.rsqrt(jnp.mean(centred * centred, -1, keepdims=True) + 1e-12)
    normed = centred * inv_std
    return normed * gain + shift, normed, inv_std


def norm_back(grad_out, normed, inv_std, gain):
    scaled = grad_out * gain
    grad_in = inv_std * (
        scaled
        - jnp.mean(scaled, -1, keepdims=True)
        - normed * jnp.mean(scaled * normed, -1, keepdims=True)
    )
    return grad_in, jnp.sum(grad_out * normed, 0), jnp.sum(grad_out, 0)


def gelu_parts(values):
    cdf = 0.5 * (1.0 + lax.erf(values * (1.0 / math.sqrt(2.0))))
    bell = jnp.exp(-0.5 * values * values) * (1.0 / math.sqrt(2.0 * math.pi))
    return values * cdf, cdf + values * bell


def gather(x):
    return lax.all_gather(x, "shard", axis=0, tiled=True)


def rep_sum(x, reps):
    step = 1
    while step < reps:
        other = lax.ppermute(x.astype(BF), "rep", [(i, i ^ step) for i in range(reps)])
        x = x.astype(BF).astype(F32) + other.astype(F32)
        step *= 2
    return x


def body(
    shards,
    reps,
    layer_input,
    segment_ids,
    cotangent,
    w_qkv,
    bias_query,
    bias_value,
    w_out,
    bias_out,
    ln1_gain,
    ln1_bias,
    w_up,
    bias_up,
    w_down,
    bias_down,
    ln2_gain,
    ln2_bias,
):
    _, length, width = layer_input.shape
    part = width // shards
    x = layer_input.reshape(length, width)
    dy = cotangent.reshape(length, width).astype(F32)
    small = jnp.concatenate(
        [bias_query, bias_value, bias_out, ln1_gain, ln1_bias, bias_down, ln2_gain, ln2_bias, bias_up]
    )[None]
    full_qkv = gather(w_qkv)
    full_small = gather(small)
    full_out = gather(w_out)
    full_up = gather(w_up)
    full_down = gather(w_down)
    vec = lambda i: full_small[:, i * part : (i + 1) * part].reshape(-1).astype(F32)
    b_query, b_value, b_out, g_one, s_one, b_down, g_two, s_two = [vec(i) for i in range(8)]
    b_up = full_small[:, 8 * part :].reshape(-1).astype(F32)
    seg = segment_ids.reshape(length)
    feat_query, feat_key = doc_features(seg)

    qkv_bias = jnp.concatenate([b_query, jnp.zeros_like(b_query), b_value])
    projected = (dot(x, full_qkv) + qkv_bias).astype(BF)
    mixed, feat_row = attn_fwd(projected, feat_query, feat_key)
    hidden = x.astype(F32) + dot(mixed, full_out) + b_out
    normed_value, normed_one, inv_one = layer_norm(hidden, g_one, s_one)
    normed_low = normed_value.astype(BF)
    inner = dot(normed_low, full_up) + b_up
    act, slope = gelu_parts(inner)
    act = act.astype(BF)
    summed = normed_low.astype(F32) + dot(act, full_down) + b_down
    out_value, normed_two, inv_two = layer_norm(summed, g_two, s_two)
    layer_output = out_value.astype(BF).reshape(1, length, width)

    d_summed, grad_g_two, grad_s_two = norm_back(dy, normed_two, inv_two, g_two)
    d_ffn = d_summed.astype(BF)
    grad_down = dot(act, d_ffn, TN).astype(BF)
    grad_b_down = jnp.sum(d_ffn.astype(F32), 0)
    d_inner = (dot(d_ffn, full_down, NT) * slope).astype(BF)
    grad_up = dot(normed_low, d_inner, TN).astype(BF)
    grad_b_up = jnp.sum(d_inner.astype(F32), 0)
    d_normed = d_summed + dot(d_inner, full_up, NT)
    d_hidden, grad_g_one, grad_s_one = norm_back(d_normed, normed_one, inv_one, g_one)
    d_attn = d_hidden.astype(BF)
    grad_out = dot(mixed, d_attn, TN).astype(BF)
    grad_b_out = jnp.sum(d_attn.astype(F32), 0)
    d_mixed = dot(d_attn, full_out, NT).astype(BF)

    d_mixed, grad_down, grad_up, grad_out = lax.optimization_barrier(
        (d_mixed, grad_down, grad_up, grad_out)
    )
    scatter = lambda g: lax.psum_scatter(g, "shard", scatter_dimension=0, tiled=True)
    own_down = scatter(grad_down)
    own_up = scatter(grad_up)
    own_out = scatter(grad_out)
    d_query, d_key, d_value = attn_bwd(projected, d_mixed, mixed, feat_row, feat_key)
    d_projected = jnp.concatenate([d_query, d_key, d_value], -1)
    grad_qkv = dot(x, d_projected, TN).astype(BF)
    grad_b_query = jnp.sum(d_query.astype(F32), 0)
    grad_b_value = jnp.sum(d_value.astype(F32), 0)
    input_grad = (d_hidden + dot(d_projected, full_qkv, NT)).astype(BF).reshape(1, length, width)

    small_grads = jnp.concatenate(
        [
            g.reshape(shards, -1)
            for g in (
                grad_b_query,
                grad_b_value,
                grad_b_out,
                grad_g_one,
                grad_s_one,
                grad_b_down,
                grad_g_two,
                grad_s_two,
                grad_b_up,
            )
        ],
        1,
    )
    count = small_grads.shape[1]
    columns = 3 * width
    rows = -(-count // (8 * columns)) * 8
    small_rows = jnp.pad(small_grads, ((0, 0), (0, rows * columns - count))).reshape(shards, rows, columns)
    packed = jnp.concatenate([grad_qkv.reshape(shards, part, columns), small_rows.astype(BF)], 1)
    own_packed = scatter(packed.reshape(shards * (part + rows), columns))

    own_down = rep_sum(own_down, reps)
    own_up = rep_sum(own_up, reps)
    own_out = rep_sum(own_out, reps)
    own_packed = rep_sum(own_packed, reps)
    own_qkv = own_packed[:part]
    own_small = own_packed[part:].reshape(-1)
    piece = lambda i: own_small[i * part : (i + 1) * part]
    return (
        layer_output,
        input_grad,
        own_qkv,
        piece(0),
        piece(1),
        own_out,
        piece(2),
        piece(3),
        piece(4),
        own_up,
        own_small[8 * part : count],
        own_down,
        piece(5),
        piece(6),
        piece(7),
    )


def solution(mesh):
    shards, reps = mesh.shape["shard"], mesh.shape["rep"]
    rows = P(("rep", "shard"), None, None)
    mat, vec = P("shard", None), P("shard")
    return jax.shard_map(
        functools.partial(body, shards, reps),
        mesh=mesh,
        in_specs=(
            rows,
            P(("rep", "shard"), None),
            rows,
            mat,
            vec,
            vec,
            mat,
            vec,
            vec,
            vec,
            mat,
            vec,
            mat,
            vec,
            vec,
            vec,
        ),
        out_specs=(rows, rows, mat, vec, vec, mat, vec, vec, vec, mat, vec, mat, vec, vec, vec),
        check_vma=False,
    )
```

time: 719 us -> 517 us (0.72)
  matrix products: 263 us -> 97.7 us
  waiting for transfers between devices: 171 us -> 257 us
  other arithmetic: 97.9 us -> 17.6 us
  Pallas kernels: 0 us -> 65.1 us
  blocking collectives: 80.8 us -> 15.9 us
  local copies, waits for them, and re-layouts: 78.5 us -> 28 us
  starting transfers between devices: 0.36 us -> 11.5 us
    dot_general x26 -> x12, matrix products: 263 us -> 97.7 us  [dot(): return lax.dot_general(a, b, dims, preferred_element_type=F32)]
    all_gather x4, waiting for transfers between devices: 0.04 us -> 89.6 us  [gather(): return lax.all_gather(x, 'shard', axis=0, tiled=True)]
    pallas_call x0 -> x2, Pallas kernels: none -> 65.1 us  [the longest x1 39.1 us: attn_bwd(): pl.pallas_call(functools.partial(bwd_kernel, bk=bk), grid=(pairs,), in_sp...]
    unnamed x2 -> x0, blocking collectives: 57.7 us -> none
    convert_element_type x23 -> x7, other arithmetic: 55.7 us -> 3.72 us  [the longest x4 3.44 us: rep_sum(): x = x.astype(BF).astype(F32) + other.astype(F32)]
    ppermute x0 -> x8, waiting for transfers between devices: none -> 31.8 us  [rep_sum(): lax.ppermute(x.astype(BF), 'rep', [(i, i ^ step) for i in range(reps)])]
    reduce_sum x5 -> x4, other arithmetic: 31.5 us -> 4.88 us  [the longest x1 2.76 us: body(): grad_b_out = jnp.sum(d_attn.astype(F32), 0)]
    unnamed x134 -> x46, local copies, waits for them, and re-layouts: 41.4 us -> 18.3 us
  transfers between devices with their start and end apart: 9 -> 16, of which waited for: 5 -> 11; matrix products, arithmetic and copies ran while one was open for 25% -> 13% of each run, Pallas kernels for 0% -> 13%
where the time goes in v1:
time: 517 us; the launch traced here: 508 us
  waiting for transfers between devices  257 us (50%)
  matrix products  97.7 us (19%)
  Pallas kernels  65.1 us (13%)
  local copies, waits for them, and re-layouts  28 us (5%)
  other arithmetic  17.6 us (3%)
  blocking collectives  15.9 us (3%)
  between operations  14.9 us (3%)
  starting transfers between devices  11.5 us (2%)
    reduce_scatter x4, waiting for transfers between devices, body(): lax.psum_scatter(g, 'shard', scatter_dimension=0, tiled=True)  132 us
    dot_general x12, matrix products, dot(): return lax.dot_general(a, b, dims, preferred_element_type=F32)  97.7 us
    all_gather x4, waiting for transfers between devices, gather(): return lax.all_gather(x, 'shard', axis=0, tiled=True)  89.6 us
    pallas_call x1, Pallas kernels, attn_bwd(): pl.pallas_call(functools.partial(bwd_kernel, bk=bk), grid=(pairs,), in_sp...  39.1 us
    ppermute x8, waiting for transfers between devices, rep_sum(): lax.ppermute(x.astype(BF), 'rep', [(i, i ^ step) for i in range(reps)])  31.8 us
    pallas_call x1, Pallas kernels, attn_fwd(): pl.pallas_call(functools.partial(fwd_kernel, bq=bq), grid=(nb,), in_specs...  26 us
    unnamed x46, local copies, waits for them, and re-layouts  18.3 us
    all_gather x1, blocking collectives, gather(): return lax.all_gather(x, 'shard', axis=0, tiled=True)  15.9 us
  transfers between devices with their start and end apart: 16, of which 11 were waited for; matrix products, arithmetic and copies ran while one was open for 13% of the time, Pallas kernels for 13%

profile of v1, /device:TPU:0, one launch (start us, length us, event | category | flops | bytes accessed | tf_op | source)
XLA Modules:
  0.0 507.8 jit_solution(5023490512175452158)
XLA Ops:
  10.0 6.1 %concatenate.16 = bf16[1152]{0:T(1024)(128)(2,1)S(1)} concatenate(bf16[96]{0:T(256)(128)(2,1)} %param.20, bf16[96]{0:T(256)(128)(2,1)} %param.21, bf16[96]{0:T(256)(128)(2,1)} %param.23, bf16[96]{0:T(256)(128)(2,1)} %param.24, bf16[96]{0:T(256)(128)(2,1)} %param.25, bf16[96]{0:T(256)(128)(2,1)} %param.29, bf16[96]{0:T(256)(128)(2,1)} %param.30, bf16[96]{0:T(256)(128)(2,1)} %param.31, ...), dimensions={0} | concatenate | bytes 4608 | tf_op jit(solution)/shard_map/concatenate | solution.py:230
  16.2 15.9 %all-gather.1 = bf16[8,1,1152]{2,1,0:T(2,128)(2,1)S(1)} all-gather(bf16[1,1,1152]{2,1,0:T(2,128)(2,1)S(1)} %reshape.217), channel_id=2, replica_groups=mesh['rep'=4,'shard'=8] {'shard'}, dimensions={0}, use_global_device_ids=true | all-gather | bytes 20736 | tf_op jit(solution)/shard_map/all_gather | solution.py:194
  32.4 2.6 copy.45
  35.3 1.6 copy.47
  37.6 16.6 %all-gather.7.cloned.1.call-done = bf16[768,2304]{1,0:T(8,128)(2,1)} async-done(((bf16[96,2304]{1,0:T(8,128)(2,1)}), bf16[768,2304]{1,0:T(8,128)(2,1)}) %all-gather.7.cloned.1.call-update) | async-done | bytes 3538960 | tf_op jit(solution)/shard_map/all_gather | solution.py:194
  54.1 8.5 %add_convert_fusion.q_ref.k_ref.v_ref = bf16[1024,2304]{1,0:T(8,128)(2,1)} fusion(bf16[768,2304]{1,0:T(8,128)(2,1)} %all-gather.7.cloned.1.call-done, f32[2304]{0:T(1024)S(1)} %pad_maximum_fusion.1, bf16[1,1024,768]{2,1,0:T(8,128)(2,1)} %param.16), kind=kOutput, calls=%fused_computation.9 | convolution fusion | flops 3628597248 | bytes 9839616 | tf_op jit(solution)/shard_map/dot_general | solution.py:21
  62.6 26.0 %attn_fwd.1 = (bf16[1024,768]{1,0:T(8,128)(2,1)S(1)}, bf16[1024,768]{1,0:T(8,128)(2,1)S(1)}) custom-call(bf16[1024,2304]{1,0:T(8,128)(2,1)} %add_convert_fusion.q_ref.k_ref.v_ref, bf16[1024,2304]{1,0:T(8,128)(2,1)} %add_convert_fusion.q_ref.k_ref.v_ref, bf16[1024,2304]{1,0:T(8,128)(2,1)} %add_convert_fusion.q_ref.k_ref.v_ref, ...), custom_call_target="tpu_custom_call" | custom-call | flops 6442450944 | bytes 7864320 | tf_op jit(solution)/shard_map/attn_fwd/pallas_call | solution.py:89
  89.7 4.0 fusion.30
  93.7 1.6 copy-done.4
  95.7 34.8 %all-gather.11.cloned.1.call-done = bf16[768,3072]{1,0:T(8,128)(2,1)} async-done(((bf16[96,3072]{1,0:T(8,128)(2,1)}), bf16[768,3072]{1,0:T(8,128)(2,1)}) %all-gather.11.cloned.1.call-update) | async-done | bytes 4718608 | tf_op jit(solution)/shard_map/all_gather | solution.py:194
  130.5 13.8 %multiply_convert_fusion = (bf16[1024,3072]{1,0:T(8,128)(2,1)}, f32[1024,3072]{1,0:T(8,128)}) fusion(f32[3072]{0:T(1024)S(1)} %reshape.212, bf16[768,3072]{1,0:T(8,128)(2,1)} %all-gather.11.cloned.1.call-done, f32[1024,768]{0,1:T(8,128)} %copy-done.4, f32[768]{0:T(1024)S(1)} %reshape.211, f32[768]{0:T(1024)S(1)} %reshape.210, f32[1024]{0:T(1024)S(1)} %add_rsqrt_fusion.1, ...), kind=kOutput, calls=%fused_computation.7 | convolution fusion | flops 4854644736 | bytes 26765312 | tf_op jit(solution)/shard_map/dot_general | solution.py:21
  144.3 38.3 %all-gather.13.cloned.1.call-done = bf16[3072,768]{1,0:T(8,128)(2,1)} async-done(((bf16[384,768]{1,0:T(8,128)(2,1)}), bf16[3072,768]{1,0:T(8,128)(2,1)}) %all-gather.13.cloned.1.call-update) | async-done | bytes 4718608 | tf_op jit(solution)/shard_map/all_gather | solution.py:194
  182.6 9.6 %fusion.31 = (f32[1024]{0:T(1024)S(1)}, f32[1024,768]{0,1:T(8,128)S(1)}) fusion(f32[768]{0:T(1024)S(1)} %reshape.213, bf16[1024,3072]{1,0:T(8,128)(2,1)} %get-tuple-element.114, bf16[3072,768]{1,0:T(8,128)(2,1)} %all-gather.13.cloned.1.call-done, f32[768]{0:T(1024)S(1)} %reshape.211, f32[768]{0:T(1024)S(1)} %reshape.210, f32[1024]{0:T(1024)S(1)} %add_rsqrt_fusion.1, ...), kind=kOutput, calls=%fused_computation.94 | convolution fusion | flops 4838915072 | bytes 17323008 | tf_op jit(solution)/shard_map/dot_general | solution.py:21
  192.6 2.1 copy-done.3
  194.7 2.6 fusion.12
  197.3 1.3 fusion.25
  199.7 6.8 %convolution_convert_fusion.1 = bf16[3072,768]{1,0:T(8,128)(2,1)} fusion(bf16[1024,3072]{1,0:T(8,128)(2,1)S(1)} %bitcast.61, bf16[1024,768]{0,1:T(8,128)(2,1)S(1)} %get-tuple-element.86), kind=kOutput, calls=%fused_computation.11 | convolution fusion | flops 4834197504 | bytes 12582912 | tf_op jit(solution)/shard_map/dot_general | solution.py:21
  206.5 12.5 %fusion.32 = (bf16[3072]{0:T(1024)(128)(2,1)S(1)}, bf16[1024,3072]{1,0:T(8,128)(2,1)S(1)}) fusion(f32[1024,3072]{1,0:T(8,128)} %get-tuple-element.115, f32[3072]{0:T(1024)S(1)} %reshape.212, bf16[1024,768]{0,1:T(8,128)(2,1)} %copy-done.10, bf16[3072,768]{1,0:T(8,128)(2,1)} %all-gather.13.cloned.1.call-done), kind=kOutput, calls=%fused_computation.95 | convolution fusion | flops 4869583872 | bytes 25184256 | tf_op jit(solution)/shard_map/dot_general | solution.py:21
  219.1 2.7 copy-done.16
  221.8 7.3 %convolution_convert_fusion = bf16[768,3072]{1,0:T(8,128)(2,1)} fusion(bf16[1024,3072]{1,0:T(8,128)(2,1)S(1)} %get-tuple-element.120, f32[1024,768]{0,1:T(8,128)S(1)} %copy-done.5, f32[768]{0:T(1024)S(1)} %reshape.211, f32[768]{0:T(1024)S(1)} %reshape.210, f32[1024]{0:T(1024)S(1)} %add_rsqrt_fusion.1, f32[1024]{0:T(1024)S(1)} %broadcast_multiply_fusion.5), kind=kOutput, calls=%fused_computation.10 | convolution fusion | flops 4838129664 | bytes 14170112 | tf_op jit(solution)/shard_map/dot_general | solution.py:21
  229.0 11.7 %multiply_reduce_fusion = (bf16[768]{0:T(1024)(128)(2,1)S(1)}, f32[1024]{0:T(1024)S(1)}, f32[1024]{0:T(1024)S(1)}, bf16[768]{0:T(1024)(128)(2,1)S(1)}, f32[1024,768]{0,1:T(8,128)S(1)}) fusion(f32[1024,768]{0,1:T(8,128)} %copy-done.4, f32[1024]{0:T(1024)S(1)} %add_rsqrt_fusion.1, f32[1024]{0:T(1024)S(1)} %broadcast_multiply_fusion.5, f32[768]{0:T(1024)S(1)} %reshape.210, ...), kind=kOutput, calls=%fused_computation.23 | convolution fusion | flops 4845989888 | bytes 22062080 | tf_op jit(solution)/shard_map/dot_general | solution.py:21
  240.8 2.8 convert_reduce_fusion
  243.6 4.4 convolution_convert_fusion.4
  248.0 4.5 convolution_convert_fusion.3.g_ref
  252.6 39.1 %attn_bwd.1 = (bf16[1024,768]{1,0:T(8,128)(2,1)S(1)}, bf16[1024,768]{1,0:T(8,128)(2,1)S(1)}, bf16[1024,768]{1,0:T(8,128)(2,1)S(1)}) custom-call(bf16[1024,2304]{1,0:T(8,128)(2,1)} %add_convert_fusion.q_ref.k_ref.v_ref, bf16[1024,2304]{1,0:T(8,128)(2,1)} %add_convert_fusion.q_ref.k_ref.v_ref, bf16[1024,2304]{1,0:T(8,128)(2,1)} %add_convert_fusion.q_ref.k_ref.v_ref, ...), custom_call_target="tpu_custom_call" | custom-call | flops 16106127360 | bytes 14155776 | tf_op jit(solution)/shard_map/attn_bwd/pallas_call | solution.py:156
  292.7 2.1 copy-done.12
  295.6 6.5 %convolution_convert_fusion.2 = bf16[2304,768]{0,1:T(8,128)(2,1)S(1)} fusion(bf16[1024,2304]{1,0:T(8,128)(2,1)} %copy-done.12, bf16[1,1024,768]{2,1,0:T(8,128)(2,1)S(1)} %copy-done.9), kind=kOutput, calls=%fused_computation.12 | convolution fusion | flops 3625648128 | bytes 9830400 | tf_op jit(solution)/shard_map/dot_general | solution.py:21
  302.1 2.1 pad_maximum_fusion
  305.7 1.5 collective-permute-start.2
  307.3 4.7 collective-permute-done.2
  313.0 1.5 collective-permute-start.3
  314.5 35.6 %reduce-scatter.5.cloned.1.call-done = bf16[104,2304]{1,0:T(8,128)(2,1)} async-done(((bf16[832,2304]{1,0:T(8,128)(2,1)}), bf16[104,2304]{1,0:T(8,128)(2,1)}) %reduce-scatter.5.cloned.1.call-update) | async-done | bytes 479248 | tf_op jit(solution)/shard_map/reduce_scatter | solution.py:274
  350.1 1.5 collective-permute-start
  351.5 8.1 %fusion.16 = bf16[1,1024,768]{1,2,0:T(8,128)(2,1)S(1)} fusion(f32[1024,768]{0,1:T(8,128)} %get-tuple-element.88, bf16[1024,2304]{1,0:T(8,128)(2,1)} %copy-done.12, bf16[768,2304]{1,0:T(8,128)(2,1)} %all-gather.7.cloned.1.call-done), kind=kOutput, calls=%fused_computation.42 | convolution fusion | flops 3625451520 | bytes 12976128 | tf_op jit(solution)/shard_map/dot_general | solution.py:21
  359.7 1.6 copy.51
  361.3 1.6 copy.50
  363.6 41.9 %reduce-scatter.11.cloned.1.call-done = bf16[384,768]{1,0:T(8,128)(2,1)} async-done(((bf16[3072,768]{1,0:T(8,128)(2,1)}), bf16[384,768]{1,0:T(8,128)(2,1)}) %reduce-scatter.11.cloned.1.call-update) | async-done | bytes 589840 | tf_op jit(solution)/shard_map/reduce_scatter | solution.py:274
  405.5 1.5 collective-permute-start.6
  407.0 54.2 %reduce-scatter.9.cloned.1.call-done = bf16[96,3072]{1,0:T(8,128)(2,1)} async-done(((bf16[768,3072]{1,0:T(8,128)(2,1)}), bf16[96,3072]{1,0:T(8,128)(2,1)}) %reduce-scatter.9.cloned.1.call-update) | async-done | bytes 589840 | tf_op jit(solution)/shard_map/reduce_scatter | solution.py:274
  461.1 1.5 collective-permute-start.4
  463.8 1.5 collective-permute-start.1
  465.3 1.2 add_convert_fusion.4
  467.1 7.1 %collective-permute-done.4 = bf16[96,3072]{1,0:T(8,128)(2,1)S(1)} collective-permute-done((bf16[96,3072]{1,0:T(8,128)(2,1)}, bf16[96,3072]{1,0:T(8,128)(2,1)S(1)}, u32[]{:S(2)}, u32[]{:S(2)}) %collective-permute-start.4) | collective-permute-done | bytes 589856 | tf_op jit(solution)/shard_map/ppermute | solution.py:200
  474.4 1.5 collective-permute-start.5
  476.0 1.8 collective-permute-done.1
  480.1 10.3 %collective-permute-done.7 = bf16[384,768]{1,0:T(8,128)(2,1)S(1)} collective-permute-done((bf16[384,768]{1,0:T(8,128)(2,1)S(1)}, bf16[384,768]{1,0:T(8,128)(2,1)S(1)}, u32[]{:S(2)}, u32[]{:S(2)}) %collective-permute-start.7) | collective-permute-done | bytes 589856 | tf_op jit(solution)/shard_map/ppermute | solution.py:200
  491.5 7.9 %collective-permute-done.5 = bf16[96,3072]{1,0:T(8,128)(2,1)S(1)} collective-permute-done((bf16[96,3072]{1,0:T(8,128)(2,1)S(1)}, bf16[96,3072]{1,0:T(8,128)(2,1)S(1)}, u32[]{:S(2)}, u32[]{:S(2)}) %collective-permute-start.5) | collective-permute-done | bytes 589856 | tf_op jit(solution)/shard_map/ppermute | solution.py:200
  499.4 1.2 convert_add_fusion.1
  (112 shorter events, 17.5 us)
Async XLA Ops:
  7.2 28.2 %copy-start.7 = (bf16[1,1024,768]{2,1,0:T(8,128)(2,1)S(1)}, bf16[1,1024,768]{2,1,0:T(8,128)(2,1)}, u32[]{:S(2)}) copy-start(bf16[1,1024,768]{2,1,0:T(8,128)(2,1)} %param.18) | copy-start | bytes 4718596
  7.2 46.9 %all-gather.7.cloned.1.call-start = ((), (), s32[]{:S(2)}) async-start(), calls=%async_computation.4 | async-start | bytes 3981312 | tf_op jit(solution)/shard_map/all_gather | solution.py:194
  7.9 81.8 %all-gather.9.cloned.1.call-start = ((), (), s32[]{:S(2)}) async-start(), calls=%async_computation.5 | async-start | bytes 1327104 | tf_op jit(solution)/shard_map/all_gather | solution.py:194
  8.7 121.8 %all-gather.11.cloned.1.call-start = ((), (), s32[]{:S(2)}) async-start(), calls=%async_computation.6 | async-start | bytes 5308416 | tf_op jit(solution)/shard_map/all_gather | solution.py:194
  9.4 173.1 %all-gather.13.cloned.1.call-start = ((), (), s32[]{:S(2)}) async-start(), calls=%async_computation.7 | async-start | bytes 5308416 | tf_op jit(solution)/shard_map/all_gather | solution.py:194
  10.0 295.7 %reduce-scatter.7.cloned.1.call-start = ((), (), s32[]{:S(2)}) async-start(), calls=%async_computation.9 | async-start | bytes 1327104 | tf_op jit(solution)/shard_map/reduce_scatter | solution.py:274
  35.0 2.4 copy-start.14
  88.6 1.1 copy-start.1
  89.7 153.9 %copy-start = (bf16[1024,768]{1,0:T(8,128)(2,1)}, bf16[1024,768]{1,0:T(8,128)(2,1)S(1)}, u32[]{:S(2)}) copy-start(bf16[1024,768]{1,0:T(8,128)(2,1)S(1)} %get-tuple-element.24.o_ref) | copy-start | bytes 4718596
  93.7 1.6 copy-start.4
  192.1 5.1 %copy-start.2 = (f32[1024,768]{0,1:T(8,128)}, f32[1024,768]{0,1:T(8,128)S(1)}, u32[]{:S(2)}) copy-start(f32[1024,768]{0,1:T(8,128)S(1)} %get-tuple-element.117) | copy-start | bytes 9437188
  192.1 2.5 copy-start.3
  192.2 7.5 %slice-start = ((s8[6291456]{0:T(1024)(128)(4,1)}), s8[4194304]{0:T(1024)(128)(4,1)S(1)}, s32[]{:S(2)}) async-start(s8[6291456]{0:T(1024)(128)(4,1)} %bitcast.60), calls=%async_computation.12 | async-start | bytes 8388608
  194.7 5.0 slice-start.1
  198.5 1.1 copy-start.10
  206.5 15.2 %copy-start.5 = (f32[1024,768]{0,1:T(8,128)S(1)}, f32[1024,768]{0,1:T(8,128)}, u32[]{:S(2)}) copy-start(f32[1024,768]{0,1:T(8,128)} %copy-done.4) | copy-start | bytes 9437188
  219.1 2.7 copy-start.16
  229.0 11.8 %copy-start.6 = (f32[1024,768]{0,1:T(8,128)S(1)}, f32[1024,768]{0,1:T(8,128)}, u32[]{:S(2)}) copy-start(f32[1024,768]{0,1:T(8,128)} %copy-done.4) | copy-start | bytes 9437188
  243.6 4.4 copy-start.15
  252.5 97.5 %reduce-scatter.5.cloned.1.call-start = ((), (), s32[]{:S(2)}) async-start(), calls=%async_computation.8 | async-start | bytes 4313088 | tf_op jit(solution)/shard_map/reduce_scatter | solution.py:274
  292.2 3.5 copy-start.9
  292.7 2.1 copy-start.12
  304.2 101.3 %reduce-scatter.11.cloned.1.call-start = ((), (), s32[]{:S(2)}) async-start(), calls=%async_computation.11 | async-start | bytes 5308416 | tf_op jit(solution)/shard_map/reduce_scatter | solution.py:274
  305.0 156.2 %reduce-scatter.9.cloned.1.call-start = ((), (), s32[]{:S(2)}) async-start(), calls=%async_computation.10 | async-start | bytes 5308416 | tf_op jit(solution)/shard_map/reduce_scatter | solution.py:274
  305.7 6.3 %collective-permute-start.2 = (bf16[96,768]{1,0:T(8,128)(2,1)}, bf16[96,768]{1,0:T(8,128)(2,1)S(1)}, u32[]{:S(2)}, u32[]{:S(2)}) collective-permute-start(bf16[96,768]{1,0:T(8,128)(2,1)} %reduce-scatter.7.cloned.1.call-done), channel_id=1, source_target_pairs={{0,8},{8,0},{16,24},{24,16},{1,9},{9,1},{17,25},{25,17},{2,10},{10... | collective-permute-start | bytes 442376 | tf_op jit(solution)/shard_map/ppermute | solution.py:200
  313.0 49.9 %collective-permute-start.3 = (bf16[96,768]{1,0:T(8,128)(2,1)S(1)}, bf16[96,768]{1,0:T(8,128)(2,1)S(1)}, u32[]{:S(2)}, u32[]{:S(2)}) collective-permute-start(bf16[96,768]{1,0:T(8,128)(2,1)S(1)} %add_convert_fusion.7), channel_id=1, source_target_pairs={{0,16},{8,24},{16,0},{24,8},{1,17},{9,25},{17,1},{25,9},{2,18},{10... | collective-permute-start | bytes 442376 | tf_op jit(solution)/shard_map/ppermute | solution.py:200
  350.1 112.6 %collective-permute-start = (bf16[104,2304]{1,0:T(8,128)(2,1)}, bf16[104,2304]{1,0:T(8,128)(2,1)}, u32[]{:S(2)}, u32[]{:S(2)}) collective-permute-start(bf16[104,2304]{1,0:T(8,128)(2,1)} %reduce-scatter.5.cloned.1.call-done), channel_id=1, source_target_pairs={{0,8},{8,0},{16,24},{24,16},{1,9},{9,1},{17,25},{25,17},{2,10},{10... | collective-permute-start | bytes 1437704 | tf_op jit(solution)/shard_map/ppermute | solution.py:200
  359.7 1.6 copy-start.8
  361.3 101.4 %copy-start.13 = (bf16[104,2304]{1,0:T(8,128)(2,1)S(1)}, bf16[104,2304]{1,0:T(8,128)(2,1)}, u32[]{:S(2)}) copy-start(bf16[104,2304]{1,0:T(8,128)(2,1)} %reduce-scatter.5.cloned.1.call-done) | copy-start | bytes 1437700
  405.5 59.8 %collective-permute-start.6 = (bf16[384,768]{1,0:T(8,128)(2,1)}, bf16[384,768]{1,0:T(8,128)(2,1)S(1)}, u32[]{:S(2)}, u32[]{:S(2)}) collective-permute-start(bf16[384,768]{1,0:T(8,128)(2,1)} %reduce-scatter.11.cloned.1.call-done), channel_id=1, source_target_pairs={{0,8},{8,0},{16,24},{24,16},{1,9},{9,1},{17,25},{25,17},{2,10},{10... | collective-permute-start | bytes 1769480 | tf_op jit(solution)/shard_map/ppermute | solution.py:200
  461.1 13.1 %copy-start.11 = (bf16[96,3072]{1,0:T(8,128)(2,1)S(1)}, bf16[96,3072]{1,0:T(8,128)(2,1)}, u32[]{:S(2)}) copy-start(bf16[96,3072]{1,0:T(8,128)(2,1)} %reduce-scatter.9.cloned.1.call-done) | copy-start | bytes 1769476
  461.1 13.1 %collective-permute-start.4 = (bf16[96,3072]{1,0:T(8,128)(2,1)}, bf16[96,3072]{1,0:T(8,128)(2,1)S(1)}, u32[]{:S(2)}, u32[]{:S(2)}) collective-permute-start(bf16[96,3072]{1,0:T(8,128)(2,1)} %reduce-scatter.9.cloned.1.call-done), channel_id=1, source_target_pairs={{0,8},{8,0},{16,24},{24,16},{1,9},{9,1},{17,25},{25,17},{2,10},{10... | collective-permute-start | bytes 1769480 | tf_op jit(solution)/shard_map/ppermute | solution.py:200
  463.8 14.0 %collective-permute-start.1 = (bf16[104,2304]{1,0:T(8,128)(2,1)S(1)}, bf16[104,2304]{1,0:T(8,128)(2,1)S(1)}, u32[]{:S(2)}, u32[]{:S(2)}) collective-permute-start(bf16[104,2304]{1,0:T(8,128)(2,1)S(1)} %add_convert_fusion.6), channel_id=1, source_target_pairs={{0,16},{8,24},{16,0},{24,8},{1,17},{9,25},{17,1},{25,9},{2,18},{10... | collective-permute-start | bytes 1437704 | tf_op jit(solution)/shard_map/ppermute | solution.py:200
  466.5 23.9 %collective-permute-start.7 = (bf16[384,768]{1,0:T(8,128)(2,1)S(1)}, bf16[384,768]{1,0:T(8,128)(2,1)S(1)}, u32[]{:S(2)}, u32[]{:S(2)}) collective-permute-start(bf16[384,768]{1,0:T(8,128)(2,1)S(1)} %add_convert_fusion.4), channel_id=1, source_target_pairs={{0,16},{8,24},{16,0},{24,8},{1,17},{9,25},{17,1},{25,9},{2,18},{10... | collective-permute-start | bytes 1769480 | tf_op jit(solution)/shard_map/ppermute | solution.py:200
  474.4 24.9 %collective-permute-start.5 = (bf16[96,3072]{1,0:T(8,128)(2,1)S(1)}, bf16[96,3072]{1,0:T(8,128)(2,1)S(1)}, u32[]{:S(2)}, u32[]{:S(2)}) collective-permute-start(bf16[96,3072]{1,0:T(8,128)(2,1)S(1)} %add_convert_fusion.5), channel_id=1, source_target_pairs={{0,16},{8,24},{16,0},{24,8},{1,17},{9,25},{17,1},{25,9},{2,18},{10... | collective-permute-start | bytes 1769480 | tf_op jit(solution)/shard_map/ppermute | solution.py:200
Sparse Core Ops, SparseCore 0:
  9.7 44.4 all-gather.6
  55.8 21.5 all-gather.8
  79.0 51.4 all-gather.10
  132.0 50.5 all-gather.12
  252.7 31.6 reduce-scatter.6
  304.3 45.6 reduce-scatter.4
  352.4 53.1 reduce-scatter.10
  407.8 53.2 reduce-scatter.8
